TPU v7x, 256 devices: a whole 4x4x8 slice. The times are simulated.
256 devices in a mesh: row: 8 (over x_lo, y), col: 32 (over z, x_hi, core).
Axes of the slice: x: 4 (x_hi: 2, x_lo: 2; x = x_hi * 2 + x_lo), y: 4, z: 8, core: 2. Of those that a mesh axis runs over, the one named last changes fastest.
Arguments:
- amplitudes: bfloat16 [32768, 4096], P('col', 'row'), may hold values from -6 to 6
- integrals: bfloat16 [4096, 8192], P('col', 'row'), may hold values from -0.25 to 0.25
- sym_mask: int32 [32, 64], replicated, may hold values from 0 to 1, as said below
Outputs:
- ladder: bfloat16 [32768, 8192], P('col', 'row')
Inputs may be any that keep to these rules, and one draw needn't show every extreme that they name: sym_mask[k, a] is 1 exactly when cd tile k and ab tile a carry the same one of 8 irreducible representations; among the 8 ab tiles of one index of row, at most 2 carry the same representation.
All inputs are finite; a program needn't handle non-finite values.
Results may differ from a plain program's by a relative error of at most 0.001.
Values may be sent and summed in bfloat16 or wider, within the bound.
No kernel may reach another device: no remote copies, remote signals or barrier semaphores. Data moves between devices by JAX's collectives and lax.ppermute only.
A program may use at most 64 MiB of HBM per device.

v0:
```python
import jax
import jax.numpy as jnp
from jax import lax
from jax.experimental import pallas as pl
from jax.experimental.pallas import tpu as pltpu
from jax.sharding import PartitionSpec as P

TILE = 128
AB = 8
PARTS = (352, 304, 368)
VMEM = pltpu.VMEM
SMEM = pltpu.SMEM
BF16 = jnp.bfloat16
barrier = lax.optimization_barrier


def spec(space):
    return pl.BlockSpec(memory_space=space)


def row_flip(value, flip):
    return lax.ppermute(value, "row", [(i, i ^ flip) for i in range(8)])


def col_flip(value, flip):
    return lax.ppermute(value, "col", [(i, i ^ flip) for i in range(32)])


def z_step(value, by):
    return lax.ppermute(
        value, "col", [(i, (i + (4 * by if i % 2 == 0 else -4 * by)) % 32) for i in range(32)]
    )


def place():
    return lax.axis_index("row"), lax.axis_index("col")


def tile_at(index):
    return pl.ds(pl.multiple_of(index * TILE, TILE), TILE)


def pack_kernel(mask_ref, v_ref, out_ref):
    r, c = place()
    first, last, found = jnp.int32(0), jnp.int32(0), jnp.int32(0)
    for j in range(AB):
        hit = mask_ref[c, r * AB + j] > 0
        first = jnp.where(jnp.logical_and(hit, found == 0), j, first)
        last = jnp.where(hit, j, last)
        found = jnp.where(hit, 1, found)
    zero = jnp.zeros((TILE, TILE), v_ref.dtype)
    out_ref[:, :TILE] = jnp.where(found > 0, v_ref[:, tile_at(first)], zero)
    out_ref[:, TILE:] = jnp.where(last != first, v_ref[:, tile_at(last)], zero)


def table_kernel(mask_ref, out_ref):
    r, _ = place()

    @pl.loop(0, 32)
    def _(k):
        first, last = jnp.int32(AB), jnp.int32(0)
        for j in range(AB):
            hit = mask_ref[k, r * AB + j] > 0
            first = jnp.where(hit, jnp.minimum(first, j), first)
            last = jnp.where(hit, j, last)
        out_ref[0, k] = jnp.where(first == AB, 0, first)
        out_ref[1, k] = last


def join_kernel(a, b, out_ref):
    n = out_ref.shape[0] // 2
    out_ref[:n] = a[...].reshape((n,) + out_ref.shape[1:])
    out_ref[n:] = b[...].reshape((n,) + out_ref.shape[1:])


def three_kernel(a, b, c, out_ref):
    for i, ref in enumerate((a, b, c)):
        out_ref[4 * i : 4 * i + 4] = ref[...]


def dense_kernel(table_ref, quad, r1, r2, r3, r4, theirs, out_ref):
    _, c = place()
    co, xh, z = lax.rem(c, 2), lax.rem(lax.div(c, 2), 2), lax.div(c, 4)
    way = 1 - 2 * co
    out_ref[...] = jnp.zeros_like(out_ref)
    for ref, core, shift in (
        (quad, co, 0),
        (r1, co, -way),
        (r2, co, -2 * way),
        (r3, co, -3 * way),
        (r4, co, 4),
        (theirs.at[0:4], 1 - co, way),
        (theirs.at[4:8], 1 - co, 2 * way),
        (theirs.at[8:12], 1 - co, 3 * way),
    ):
        plane = lax.rem(z + shift + 8, 8)
        for j in range(4):
            k = plane * 4 + (xh ^ (j & 1)) * 2 + (core ^ (j >> 1))
            rows = tile_at(k)
            out_ref[rows, tile_at(table_ref[1, k])] = ref[j, :, TILE:]
            out_ref[rows, tile_at(table_ref[0, k])] = ref[j, :, :TILE]


def block_rows(dense_ref, flip):
    z = place()[0] ^ flip
    return dense_ref.at[pl.ds(pl.multiple_of(z * 512, 512), 512)]


def dot(a, b):
    return jnp.dot(a, b, preferred_element_type=jnp.float32)


def total(ts, blocks, cols):
    return sum(dot(t[...], block[:, cols]) for t, block in zip(ts, blocks))


def first_kernel(dense_ref, own, p1, q1, w1, acc_ref):
    blocks = [block_rows(dense_ref, flip) for flip in (0, 4, 1, 3)]
    for col in (0, 512):
        cols = slice(col, col + 512)
        acc_ref[:, cols] = total((own, p1, q1, w1), blocks, cols)


def second_kernel(dense_ref, acc_in, pw, qp, wq, acc_ref):
    blocks = [block_rows(dense_ref, flip) for flip in (7, 5, 2)]
    for col in (0, 512):
        cols = slice(col, col + 512)
        acc_ref[:, cols] = acc_in[:, cols] + total((pw, qp, wq), blocks, cols)


def third_kernel(dense_ref, acc_ref, ta, tb, tc, out_ref, held, sems):
    block = block_rows(dense_ref, 6)
    copies = []
    for col in (0, 512):
        cols = slice(col, col + 512)
        base = 0
        for t_ref, n in zip((ta, tb, tc), PARTS):
            rows = slice(base, base + n)
            held[rows, cols] = (acc_ref[rows, cols] + dot(t_ref[...], block[:, cols])).astype(held.dtype)
            copy = pltpu.make_async_copy(held.at[rows, cols], out_ref.at[rows, cols], sems.at[len(copies)])
            copy.start()
            copies.append(copy)
            base += n
    for copy in copies:
        copy.wait()


def call(kernel, args, shape, dtype, name, table=False, out_space=VMEM, flops=1000, limit=8, **more):
    return pl.pallas_call(
        kernel,
        in_specs=[spec(SMEM)] * table + [spec(VMEM)] * (len(args) - table),
        out_specs=spec(out_space),
        out_shape=jax.ShapeDtypeStruct(shape, dtype),
        compiler_params=pltpu.CompilerParams(vmem_limit_bytes=limit * 1024 * 1024),
        cost_estimate=pl.CostEstimate(flops=flops, bytes_accessed=1000, transcendentals=0),
        name=name,
        **more,
    )(*args)


def shards(amps, integrals, sym_mask):
    q1, w1 = row_flip(amps, 1), row_flip(amps, 3)
    packed = call(
        pack_kernel, (sym_mask, integrals), (TILE, 2 * TILE), BF16, "pack", table=True, limit=60
    )
    table = call(table_kernel, (sym_mask,), (2, 32), jnp.int32, "table", table=True, out_space=SMEM)

    sent, packed = barrier((amps, packed))
    p1 = row_flip(sent, 4)
    pair = call(join_kernel, (packed, col_flip(packed, 2)), (2, TILE, 2 * TILE), BF16, "pair", flops=20000000000)
    quad = call(join_kernel, (pair, col_flip(pair, 1)), (4, TILE, 2 * TILE), BF16, "quad")
    r1, r2 = z_step(quad, 1), z_step(quad, 2)
    p1, q1, w1 = barrier((p1, q1, w1))
    r3, r4 = z_step(r2, 1), z_step(r2, 2)
    theirs = col_flip(call(three_kernel, (r1, r2, r3), (12, TILE, 2 * TILE), BF16, "three"), 1)
    dense = call(
        dense_kernel, (table, quad, r1, r2, r3, r4, theirs), (4096, 1024), BF16, "dense", table=True, flops=2000000000
    )

    pw, qp, wq = row_flip(w1, 4), row_flip(p1, 1), row_flip(q1, 3)
    acc = call(first_kernel, (dense, amps, p1, q1, w1), (1024, 1024), jnp.float32, "first")
    wq, pw, qp = (barrier((acc, v))[1] for v in (wq, pw, qp))
    a, b, _ = PARTS
    last = (row_flip(wq[:a], 4), row_flip(pw[a : a + b], 1), row_flip(qp[a + b :], 3))
    acc = call(
        second_kernel, (dense, acc, pw, qp, wq), (1024, 1024), jnp.float32, "second",
        input_output_aliases={1: 0},
    )
    return call(
        third_kernel, (dense, acc, *last), (1024, 1024), BF16, "third", out_space=pl.ANY,
        scratch_shapes=[VMEM((1024, 1024), BF16), pltpu.SemaphoreType.DMA((6,))],
    )


def solution(mesh):
    placed = (P("col", "row"), P("col", "row"), P())
    return jax.shard_map(
        shards, mesh=mesh, in_specs=placed, out_specs=P("col", "row"), check_vma=False
    )
```

profile of v0, /device:TPU:64, one launch (start us, length us, event | category | flops | bytes accessed | tf_op | source)
XLA Modules:
  0.0 68.0 jit_solution(16851593079879365959)
XLA Ops:
  0.0 0.0 copy-start.2
  0.0 1.7 %pack.1.a = bf16[128,256]{1,0:T(8,128)(2,1)} custom-call(s32[32,64]{1,0:T(8,128)} %mask_ref.3, bf16[128,1024]{1,0:T(8,128)(2,1)} %v_ref.1), custom_call_target="tpu_custom_call" | custom-call | flops 1000 | bytes 1000 | tf_op jit(solution)/shard_map/pack/pallas_call | solution.py:149
  1.7 3.0 %collective-permute-start = (bf16[128,256]{1,0:T(8,128)(2,1)}, bf16[128,256]{1,0:T(8,128)(2,1)S(1)}, u32[]{:S(2)}, u32[]{:S(2)}) collective-permute-start(bf16[128,256]{1,0:T(8,128)(2,1)} %pack.1.a), channel_id=1, source_target_pairs={{0,2},{1,3},{2,0},{3,1},{4,6},{5,7},{6,4},{7,5},{8,10},{9,11},{10,... | collective-permute-start | bytes 196616 | tf_op jit(solution)/shard_map/ppermute | solution.py:26
  4.8 1.6 %collective-permute-start.8 = (bf16[1024,512]{1,0:T(8,128)(2,1)}, bf16[1024,512]{1,0:T(8,128)(2,1)S(1)}, u32[]{:S(2)}, u32[]{:S(2)}) collective-permute-start(bf16[1024,512]{1,0:T(8,128)(2,1)} %own.1), channel_id=1, source_target_pairs={{0,32},{32,0},{64,96},{96,64},{128,160},{160,128},{192,224},{224,1... | collective-permute-start | bytes 3145736 | tf_op jit(solution)/shard_map/ppermute | solution.py:22
  6.3 2.2 %collective-permute-start.9 = (bf16[1024,512]{1,0:T(8,128)(2,1)}, bf16[1024,512]{1,0:T(8,128)(2,1)S(1)}, u32[]{:S(2)}, u32[]{:S(2)}) collective-permute-start(bf16[1024,512]{1,0:T(8,128)(2,1)} %own.1), channel_id=1, source_target_pairs={{0,96},{32,64},{64,32},{96,0},{128,224},{160,192},{192,160},{224,1... | collective-permute-start | bytes 3145736 | tf_op jit(solution)/shard_map/ppermute | solution.py:22
  8.5 0.6 collective-permute-start.7
  9.1 0.0 collective-permute-done.b
  9.1 0.0 copy-start.1
  9.1 0.8 %copy-done.1 = bf16[128,256]{1,0:T(8,128)(2,1)S(1)} copy-done((bf16[128,256]{1,0:T(8,128)(2,1)S(1)}, bf16[128,256]{1,0:T(8,128)(2,1)}, u32[]{:S(2)}) %copy-start.1) | copy-done | bytes 65560
  10.0 0.1 collective-permute-start.1
  10.1 1.3 %collective-permute-done.1.b = bf16[2,128,256]{2,1,0:T(8,128)(2,1)S(1)} collective-permute-done((bf16[2,128,256]{2,1,0:T(8,128)(2,1)S(1)}, bf16[2,128,256]{2,1,0:T(8,128)(2,1)S(1)}, u32[]{:S(2)}, u32[]{:S(2)}) %collective-permute-start.1) | collective-permute-done | bytes 131104 | tf_op jit(solution)/shard_map/ppermute | solution.py:26
  11.4 4.6 %collective-permute-start.3 = (bf16[4,128,256]{2,1,0:T(8,128)(2,1)S(1)}, bf16[4,128,256]{2,1,0:T(8,128)(2,1)S(1)}, u32[]{:S(2)}, u32[]{:S(2)}) collective-permute-start(bf16[4,128,256]{2,1,0:T(8,128)(2,1)S(1)} %quad.1), channel_id=1, source_target_pairs={{0,8},{1,25},{2,10},{3,27},{4,12},{5,29},{6,14},{7,31},{8,16},{9,1... | collective-permute-start | bytes 786440 | tf_op jit(solution)/shard_map/ppermute | solution.py:30
  16.0 1.0 %collective-permute-start.2 = (bf16[4,128,256]{2,1,0:T(8,128)(2,1)S(1)}, bf16[4,128,256]{2,1,0:T(8,128)(2,1)S(1)}, u32[]{:S(2)}, u32[]{:S(2)}) collective-permute-start(bf16[4,128,256]{2,1,0:T(8,128)(2,1)S(1)} %quad.1), channel_id=1, source_target_pairs={{0,4},{1,29},{2,6},{3,31},{4,8},{5,1},{6,10},{7,3},{8,12},{9,5},{1... | collective-permute-start | bytes 786440 | tf_op jit(solution)/shard_map/ppermute | solution.py:30
  17.0 5.6 %collective-permute-done.3.b.r2 = bf16[4,128,256]{2,1,0:T(8,128)(2,1)S(1)} collective-permute-done((bf16[4,128,256]{2,1,0:T(8,128)(2,1)S(1)}, bf16[4,128,256]{2,1,0:T(8,128)(2,1)S(1)}, u32[]{:S(2)}, u32[]{:S(2)}) %collective-permute-start.3) | collective-permute-done | bytes 262176 | tf_op jit(solution)/shard_map/ppermute | solution.py:30
  22.6 0.5 collective-permute-start.4
  23.2 9.6 %collective-permute-done.7.p1 = bf16[1024,512]{1,0:T(8,128)(2,1)S(1)} collective-permute-done((bf16[1024,512]{1,0:T(8,128)(2,1)}, bf16[1024,512]{1,0:T(8,128)(2,1)S(1)}, u32[]{:S(2)}, u32[]{:S(2)}) %collective-permute-start.7) | collective-permute-done | bytes 1048608 | tf_op jit(solution)/shard_map/ppermute | solution.py:22
  32.8 0.0 collective-permute-done.8.q1
  32.8 0.0 collective-permute-done.9.w1
  32.8 0.7 collective-permute-start.11
  33.5 0.9 %collective-permute-start.12 = (bf16[1024,512]{1,0:T(8,128)(2,1)S(1)}, bf16[1024,512]{1,0:T(8,128)(2,1)S(1)}, u32[]{:S(2)}, u32[]{:S(2)}) collective-permute-start(bf16[1024,512]{1,0:T(8,128)(2,1)S(1)} %collective-permute-done.8.q1), channel_id=1, source_target_pairs={{0,96},{32,64},{64,32},{96,0},{128,224},{160,192},{192,160},{224,1... | collective-permute-start | bytes 3145736 | tf_op jit(solution)/shard_map/ppermute | solution.py:22
  34.4 1.1 %collective-permute-start.10 = (bf16[1024,512]{1,0:T(8,128)(2,1)S(1)}, bf16[1024,512]{1,0:T(8,128)(2,1)S(1)}, u32[]{:S(2)}, u32[]{:S(2)}) collective-permute-start(bf16[1024,512]{1,0:T(8,128)(2,1)S(1)} %collective-permute-done.9.w1), channel_id=1, source_target_pairs={{0,128},{32,160},{64,192},{96,224},{128,0},{160,32},{192,64},{224,... | collective-permute-start | bytes 3145736 | tf_op jit(solution)/shard_map/ppermute | solution.py:22
  35.5 0.0 collective-permute-done.2.a.r1
  35.5 0.0 collective-permute-done.4.c.r3
  35.5 0.1 three.1
  35.5 0.1 collective-permute-start.6
  35.6 4.6 %collective-permute-start.5 = (bf16[4,128,256]{2,1,0:T(8,128)(2,1)S(1)}, bf16[4,128,256]{2,1,0:T(8,128)(2,1)S(1)}, u32[]{:S(2)}, u32[]{:S(2)}) collective-permute-start(bf16[4,128,256]{2,1,0:T(8,128)(2,1)S(1)} %collective-permute-done.3.b.r2), channel_id=1, source_target_pairs={{0,8},{1,25},{2,10},{3,27},{4,12},{5,29},{6,14},{7,31},{8,16},{9,1... | collective-permute-start | bytes 786440 | tf_op jit(solution)/shard_map/ppermute | solution.py:30
  40.2 0.0 copy-done.2
  40.2 2.5 %table.1.table_ref = s32[2,32]{1,0:T(2,128)S(1)} custom-call(s32[32,64]{1,0:T(8,128)S(1)} %copy-done.2), custom_call_target="tpu_custom_call" | custom-call | flops 1000 | bytes 1000 | tf_op jit(solution)/shard_map/table/pallas_call | solution.py:149
  42.7 0.0 copy-start
  42.7 4.1 %collective-permute-done.5.r4 = bf16[4,128,256]{2,1,0:T(8,128)(2,1)S(1)} collective-permute-done((bf16[4,128,256]{2,1,0:T(8,128)(2,1)S(1)}, bf16[4,128,256]{2,1,0:T(8,128)(2,1)S(1)}, u32[]{:S(2)}, u32[]{:S(2)}) %collective-permute-start.5) | collective-permute-done | bytes 262176 | tf_op jit(solution)/shard_map/ppermute | solution.py:30
  46.8 0.0 collective-permute-done.6.theirs
  46.8 1.7 %dense.1.dense_ref = bf16[4096,1024]{1,0:T(8,128)(2,1)S(1)} custom-call(s32[2,32]{1,0:T(2,128)S(1)} %table.1.table_ref, bf16[4,128,256]{2,1,0:T(8,128)(2,1)S(1)} %quad.1, bf16[4,128,256]{2,1,0:T(8,128)(2,1)S(1)} %collective-permute-done.2.a.r1, bf16[4,128,256]{2,1,0:T(8,128)(2,1)S(1)} %collective-permute-done.3.b.r2, ...), custom_call_target="tpu_custom_call" | custom-call | flops 2000000000 | bytes 1000 | tf_op jit(solution)/shard_map/dense/pallas_call | solution.py:149
  48.5 0.0 copy-done
  48.6 4.5 %first.1.acc_in = f32[1024,1024]{1,0:T(8,128)S(1)} custom-call(bf16[4096,1024]{1,0:T(8,128)(2,1)S(1)} %dense.1.dense_ref, bf16[1024,512]{1,0:T(8,128)(2,1)S(1)} %copy-done, bf16[1024,512]{1,0:T(8,128)(2,1)S(1)} %collective-permute-done.7.p1, bf16[1024,512]{1,0:T(8,128)(2,1)S(1)} %collective-permute-done.8.q1, bf16[1024,512]{1,0:T(8,128)(2,1)S(1)} %collective-permute-done.9.w1), custom_call_target="tpu_custom_call" | custom-call | flops 1000 | bytes 1000 | tf_op jit(solution)/shard_map/first/pallas_call | solution.py:149
  53.1 2.9 %collective-permute-done.11.qp = bf16[1024,512]{1,0:T(8,128)(2,1)S(1)} collective-permute-done((bf16[1024,512]{1,0:T(8,128)(2,1)S(1)}, bf16[1024,512]{1,0:T(8,128)(2,1)S(1)}, u32[]{:S(2)}, u32[]{:S(2)}) %collective-permute-start.11) | collective-permute-done | bytes 1048608 | tf_op jit(solution)/shard_map/ppermute | solution.py:22
  56.0 1.8 %collective-permute-start.15 = (bf16[368,512]{1,0:T(8,128)(2,1)S(1)}, bf16[368,512]{1,0:T(8,128)(2,1)S(1)}, u32[]{:S(2)}, u32[]{:S(2)}) collective-permute-start(bf16[368,512]{1,0:T(8,128)(2,1)S(1)} %slice.11), channel_id=1, source_target_pairs={{0,96},{32,64},{64,32},{96,0},{128,224},{160,192},{192,160},{224,1... | collective-permute-start | bytes 1130504 | tf_op jit(solution)/shard_map/ppermute | solution.py:22
  57.8 0.1 collective-permute-done.12.wq
  57.9 0.8 %collective-permute-start.13 = (bf16[352,512]{1,0:T(8,128)(2,1)S(1)}, bf16[352,512]{1,0:T(8,128)(2,1)S(1)}, u32[]{:S(2)}, u32[]{:S(2)}) collective-permute-start(bf16[352,512]{1,0:T(8,128)(2,1)S(1)} %slice.9), channel_id=1, source_target_pairs={{0,128},{32,160},{64,192},{96,224},{128,0},{160,32},{192,64},{224,... | collective-permute-start | bytes 1081352 | tf_op jit(solution)/shard_map/ppermute | solution.py:22
  58.7 0.0 collective-permute-done.10.pw
  58.7 0.6 collective-permute-start.14
  59.3 3.5 %second.1.acc_ref = f32[1024,1024]{1,0:T(8,128)S(1)} custom-call(bf16[4096,1024]{1,0:T(8,128)(2,1)S(1)} %dense.1.dense_ref, f32[1024,1024]{1,0:T(8,128)S(1)} %first.1.acc_in, bf16[1024,512]{1,0:T(8,128)(2,1)S(1)} %collective-permute-done.10.pw, bf16[1024,512]{1,0:T(8,128)(2,1)S(1)} %collective-permute-done.11.qp, ...), custom_call_target="tpu_custom_call", output_to_operand_aliasing={{}: (1, {})} | custom-call | flops 1000 | bytes 1000 | tf_op jit(solution)/shard_map/second/pallas_call | solution.py:149
  62.9 2.8 %collective-permute-done.14.tb = bf16[304,512]{1,0:T(8,128)(2,1)S(1)} collective-permute-done((bf16[304,512]{1,0:T(8,128)(2,1)S(1)}, bf16[304,512]{1,0:T(8,128)(2,1)S(1)}, u32[]{:S(2)}, u32[]{:S(2)}) %collective-permute-start.14) | collective-permute-done | bytes 311328 | tf_op jit(solution)/shard_map/ppermute | solution.py:22
  65.7 0.0 collective-permute-done.13.ta
  65.7 0.0 collective-permute-done.15.tc
  65.7 2.1 %third.1 = bf16[1024,1024]{1,0:T(8,128)(2,1)} custom-call(bf16[4096,1024]{1,0:T(8,128)(2,1)S(1)} %dense.1.dense_ref, f32[1024,1024]{1,0:T(8,128)S(1)} %second.1.acc_ref, bf16[352,512]{1,0:T(8,128)(2,1)S(1)} %collective-permute-done.13.ta, bf16[304,512]{1,0:T(8,128)(2,1)S(1)} %collective-permute-done.14.tb, bf16[368,512]{1,0:T(8,128)(2,1)S(1)} %collective-permute-done.15.tc), custom_call_target="tpu_custom_call" | custom-call | flops 1000 | bytes 1000 | tf_op jit(solution)/shard_map/third/pallas_call | solution.py:149
  (5 shorter events, 0.1 us)
Async XLA Ops:
  0.0 40.2 %copy-start.2 = (s32[32,64]{1,0:T(8,128)S(1)}, s32[32,64]{1,0:T(8,128)}, u32[]{:S(2)}) copy-start(s32[32,64]{1,0:T(8,128)} %mask_ref.3) | copy-start | bytes 24580
  1.7 7.4 %collective-permute-start = (bf16[128,256]{1,0:T(8,128)(2,1)}, bf16[128,256]{1,0:T(8,128)(2,1)S(1)}, u32[]{:S(2)}, u32[]{:S(2)}) collective-permute-start(bf16[128,256]{1,0:T(8,128)(2,1)} %pack.1.a), channel_id=1, source_target_pairs={{0,2},{1,3},{2,0},{3,1},{4,6},{5,7},{6,4},{7,5},{8,10},{9,11},{10,... | collective-permute-start | bytes 196616 | tf_op jit(solution)/shard_map/ppermute | solution.py:26
  4.8 28.0 %collective-permute-start.8 = (bf16[1024,512]{1,0:T(8,128)(2,1)}, bf16[1024,512]{1,0:T(8,128)(2,1)S(1)}, u32[]{:S(2)}, u32[]{:S(2)}) collective-permute-start(bf16[1024,512]{1,0:T(8,128)(2,1)} %own.1), channel_id=1, source_target_pairs={{0,32},{32,0},{64,96},{96,64},{128,160},{160,128},{192,224},{224,1... | collective-permute-start | bytes 3145736 | tf_op jit(solution)/shard_map/ppermute | solution.py:22
  6.3 26.5 %collective-permute-start.9 = (bf16[1024,512]{1,0:T(8,128)(2,1)}, bf16[1024,512]{1,0:T(8,128)(2,1)S(1)}, u32[]{:S(2)}, u32[]{:S(2)}) collective-permute-start(bf16[1024,512]{1,0:T(8,128)(2,1)} %own.1), channel_id=1, source_target_pairs={{0,96},{32,64},{64,32},{96,0},{128,224},{160,192},{192,160},{224,1... | collective-permute-start | bytes 3145736 | tf_op jit(solution)/shard_map/ppermute | solution.py:22
  8.5 24.3 %collective-permute-start.7 = (bf16[1024,512]{1,0:T(8,128)(2,1)}, bf16[1024,512]{1,0:T(8,128)(2,1)S(1)}, u32[]{:S(2)}, u32[]{:S(2)}) collective-permute-start(bf16[1024,512]{1,0:T(8,128)(2,1)} %own.1), channel_id=1, source_target_pairs={{0,128},{32,160},{64,192},{96,224},{128,0},{160,32},{192,64},{224,... | collective-permute-start | bytes 3145736 | tf_op jit(solution)/shard_map/ppermute | solution.py:22
  9.1 0.8 %copy-start.1 = (bf16[128,256]{1,0:T(8,128)(2,1)S(1)}, bf16[128,256]{1,0:T(8,128)(2,1)}, u32[]{:S(2)}) copy-start(bf16[128,256]{1,0:T(8,128)(2,1)} %pack.1.a) | copy-start | bytes 196612
  10.0 1.4 %collective-permute-start.1 = (bf16[2,128,256]{2,1,0:T(8,128)(2,1)S(1)}, bf16[2,128,256]{2,1,0:T(8,128)(2,1)S(1)}, u32[]{:S(2)}, u32[]{:S(2)}) collective-permute-start(bf16[2,128,256]{2,1,0:T(8,128)(2,1)S(1)} %pair.1.a), channel_id=1, source_target_pairs={{0,1},{1,0},{2,3},{3,2},{4,5},{5,4},{6,7},{7,6},{8,9},{9,8},{10,11... | collective-permute-start | bytes 393224 | tf_op jit(solution)/shard_map/ppermute | solution.py:26
  11.4 11.2 %collective-permute-start.3 = (bf16[4,128,256]{2,1,0:T(8,128)(2,1)S(1)}, bf16[4,128,256]{2,1,0:T(8,128)(2,1)S(1)}, u32[]{:S(2)}, u32[]{:S(2)}) collective-permute-start(bf16[4,128,256]{2,1,0:T(8,128)(2,1)S(1)} %quad.1), channel_id=1, source_target_pairs={{0,8},{1,25},{2,10},{3,27},{4,12},{5,29},{6,14},{7,31},{8,16},{9,1... | collective-permute-start | bytes 786440 | tf_op jit(solution)/shard_map/ppermute | solution.py:30
  16.0 19.5 %collective-permute-start.2 = (bf16[4,128,256]{2,1,0:T(8,128)(2,1)S(1)}, bf16[4,128,256]{2,1,0:T(8,128)(2,1)S(1)}, u32[]{:S(2)}, u32[]{:S(2)}) collective-permute-start(bf16[4,128,256]{2,1,0:T(8,128)(2,1)S(1)} %quad.1), channel_id=1, source_target_pairs={{0,4},{1,29},{2,6},{3,31},{4,8},{5,1},{6,10},{7,3},{8,12},{9,5},{1... | collective-permute-start | bytes 786440 | tf_op jit(solution)/shard_map/ppermute | solution.py:30
  22.6 12.8 %collective-permute-start.4 = (bf16[4,128,256]{2,1,0:T(8,128)(2,1)S(1)}, bf16[4,128,256]{2,1,0:T(8,128)(2,1)S(1)}, u32[]{:S(2)}, u32[]{:S(2)}) collective-permute-start(bf16[4,128,256]{2,1,0:T(8,128)(2,1)S(1)} %collective-permute-done.3.b.r2), channel_id=1, source_target_pairs={{0,4},{1,29},{2,6},{3,31},{4,8},{5,1},{6,10},{7,3},{8,12},{9,5},{1... | collective-permute-start | bytes 786440 | tf_op jit(solution)/shard_map/ppermute | solution.py:30
  32.8 23.1 %collective-permute-start.11 = (bf16[1024,512]{1,0:T(8,128)(2,1)S(1)}, bf16[1024,512]{1,0:T(8,128)(2,1)S(1)}, u32[]{:S(2)}, u32[]{:S(2)}) collective-permute-start(bf16[1024,512]{1,0:T(8,128)(2,1)S(1)} %collective-permute-done.7.p1), channel_id=1, source_target_pairs={{0,32},{32,0},{64,96},{96,64},{128,160},{160,128},{192,224},{224,1... | collective-permute-start | bytes 3145736 | tf_op jit(solution)/shard_map/ppermute | solution.py:22
  33.5 24.4 %collective-permute-start.12 = (bf16[1024,512]{1,0:T(8,128)(2,1)S(1)}, bf16[1024,512]{1,0:T(8,128)(2,1)S(1)}, u32[]{:S(2)}, u32[]{:S(2)}) collective-permute-start(bf16[1024,512]{1,0:T(8,128)(2,1)S(1)} %collective-permute-done.8.q1), channel_id=1, source_target_pairs={{0,96},{32,64},{64,32},{96,0},{128,224},{160,192},{192,160},{224,1... | collective-permute-start | bytes 3145736 | tf_op jit(solution)/shard_map/ppermute | solution.py:22
  34.4 24.3 %collective-permute-start.10 = (bf16[1024,512]{1,0:T(8,128)(2,1)S(1)}, bf16[1024,512]{1,0:T(8,128)(2,1)S(1)}, u32[]{:S(2)}, u32[]{:S(2)}) collective-permute-start(bf16[1024,512]{1,0:T(8,128)(2,1)S(1)} %collective-permute-done.9.w1), channel_id=1, source_target_pairs={{0,128},{32,160},{64,192},{96,224},{128,0},{160,32},{192,64},{224,... | collective-permute-start | bytes 3145736 | tf_op jit(solution)/shard_map/ppermute | solution.py:22
  35.5 11.3 %collective-permute-start.6 = (bf16[12,128,256]{2,1,0:T(8,128)(2,1)S(1)}, bf16[12,128,256]{2,1,0:T(8,128)(2,1)S(1)}, u32[]{:S(2)}, u32[]{:S(2)}) collective-permute-start(bf16[12,128,256]{2,1,0:T(8,128)(2,1)S(1)} %three.1), channel_id=1, source_target_pairs={{0,1},{1,0},{2,3},{3,2},{4,5},{5,4},{6,7},{7,6},{8,9},{9,8},{10,11... | collective-permute-start | bytes 2359304 | tf_op jit(solution)/shard_map/ppermute | solution.py:26
  35.6 11.2 %collective-permute-start.5 = (bf16[4,128,256]{2,1,0:T(8,128)(2,1)S(1)}, bf16[4,128,256]{2,1,0:T(8,128)(2,1)S(1)}, u32[]{:S(2)}, u32[]{:S(2)}) collective-permute-start(bf16[4,128,256]{2,1,0:T(8,128)(2,1)S(1)} %collective-permute-done.3.b.r2), channel_id=1, source_target_pairs={{0,8},{1,25},{2,10},{3,27},{4,12},{5,29},{6,14},{7,31},{8,16},{9,1... | collective-permute-start | bytes 786440 | tf_op jit(solution)/shard_map/ppermute | solution.py:30
  42.7 5.9 %copy-start = (bf16[1024,512]{1,0:T(8,128)(2,1)S(1)}, bf16[1024,512]{1,0:T(8,128)(2,1)}, u32[]{:S(2)}) copy-start(bf16[1024,512]{1,0:T(8,128)(2,1)} %own.1) | copy-start | bytes 3145732
  56.0 9.8 %collective-permute-start.15 = (bf16[368,512]{1,0:T(8,128)(2,1)S(1)}, bf16[368,512]{1,0:T(8,128)(2,1)S(1)}, u32[]{:S(2)}, u32[]{:S(2)}) collective-permute-start(bf16[368,512]{1,0:T(8,128)(2,1)S(1)} %slice.11), channel_id=1, source_target_pairs={{0,96},{32,64},{64,32},{96,0},{128,224},{160,192},{192,160},{224,1... | collective-permute-start | bytes 1130504 | tf_op jit(solution)/shard_map/ppermute | solution.py:22
  57.9 7.8 %collective-permute-start.13 = (bf16[352,512]{1,0:T(8,128)(2,1)S(1)}, bf16[352,512]{1,0:T(8,128)(2,1)S(1)}, u32[]{:S(2)}, u32[]{:S(2)}) collective-permute-start(bf16[352,512]{1,0:T(8,128)(2,1)S(1)} %slice.9), channel_id=1, source_target_pairs={{0,128},{32,160},{64,192},{96,224},{128,0},{160,32},{192,64},{224,... | collective-permute-start | bytes 1081352 | tf_op jit(solution)/shard_map/ppermute | solution.py:22
  58.7 7.0 %collective-permute-start.14 = (bf16[304,512]{1,0:T(8,128)(2,1)S(1)}, bf16[304,512]{1,0:T(8,128)(2,1)S(1)}, u32[]{:S(2)}, u32[]{:S(2)}) collective-permute-start(bf16[304,512]{1,0:T(8,128)(2,1)S(1)} %slice.10), channel_id=1, source_target_pairs={{0,32},{32,0},{64,96},{96,64},{128,160},{160,128},{192,224},{224,1... | collective-permute-start | bytes 933896 | tf_op jit(solution)/shard_map/ppermute | solution.py:22
where the time goes:
time: 69.2 us; the launch traced here: 68 us
  waiting for transfers between devices  26.5 us (38%)
  starting transfers between devices  24.1 us (35%)
  Pallas kernels  16.2 us (23%)
  local copies, waits for them, and re-layouts  0.92 us (1%)
    pallas_call x9, Pallas kernels, call(): pl.pallas_call(kernel, in_specs=[spec(SMEM)] * table + [spec(VMEM)] * (le...  16.2 us
    ppermute x9, waiting for transfers between devices, row_flip(): return lax.ppermute(value, 'row', [(i, i ^ flip) for i in range(8)])  15.4 us
    ppermute x4, starting transfers between devices, z_step(): lax.ppermute(value, 'col', [(i, (i + (4 * by if i % 2 == 0 else -4 * by))...  10.7 us
    ppermute x9, starting transfers between devices, row_flip(): return lax.ppermute(value, 'row', [(i, i ^ flip) for i in range(8)])  10.3 us
    ppermute x4, waiting for transfers between devices, z_step(): lax.ppermute(value, 'col', [(i, (i + (4 * by if i % 2 == 0 else -4 * by))...  9.74 us
    ppermute x3, starting transfers between devices, col_flip(): return lax.ppermute(value, 'col', [(i, i ^ flip) for i in range(32)])  3.21 us
  transfers between devices with their start and end apart: 16, of which 7 were waited for; matrix products, arithmetic and copies ran while one was open for 0% of the time, Pallas kernels for 18%

commit v1 on v0

--- a/solution.py
+++ b/solution.py
@@ -169,9 +169,9 @@
     p1 = row_flip(sent, 4)
     pair = call(join_kernel, (packed, col_flip(packed, 2)), (2, TILE, 2 * TILE), BF16, "pair", flops=20000000000)
     quad = call(join_kernel, (pair, col_flip(pair, 1)), (4, TILE, 2 * TILE), BF16, "quad")
-    r1, r2 = z_step(quad, 1), z_step(quad, 2)
+    r1, r2 = barrier((z_step(quad, 1), z_step(quad, 2)))
     p1, q1, w1 = barrier((p1, q1, w1))
-    r3, r4 = z_step(r2, 1), z_step(r2, 2)
+    r3, r4 = barrier((z_step(r2, 1), z_step(r2, 2)))
     theirs = col_flip(call(three_kernel, (r1, r2, r3), (12, TILE, 2 * TILE), BF16, "three"), 1)
     dense = call(
         dense_kernel, (table, quad, r1, r2, r3, r4, theirs), (4096, 1024), BF16, "dense", table=True, flops=2000000000

time: 69.2 us -> 68.3 us (0.987); the launches traced: 68 us -> 68.2 us
  waiting for transfers between devices: 26.5 us -> 27.6 us
  starting transfers between devices: 24.1 us -> 23.2 us
    ppermute x4, waiting for transfers between devices: 9.74 us -> 12 us  [z_step(): lax.ppermute(value, 'col', [(i, (i + (4 * by if i % 2 == 0 else -4 * by))...]
    ppermute x9, waiting for transfers between devices: 15.4 us -> 14.2 us  [row_flip(): return lax.ppermute(value, 'row', [(i, i ^ flip) for i in range(8)])]
    ppermute x4, starting transfers between devices: 10.7 us -> 9.78 us  [z_step(): lax.ppermute(value, 'col', [(i, (i + (4 * by if i % 2 == 0 else -4 * by))...]
  transfers between devices with their start and end apart: 16 -> 16, of which waited for: 7 -> 9; matrix products, arithmetic and copies ran while one was open for 0% -> 0% of each run, Pallas kernels for 18% -> 18%
where the time goes in v1:
time: 68.3 us; the launch traced here: 68.2 us
  waiting for transfers between devices  27.6 us (40%)
  starting transfers between devices  23.2 us (34%)
  Pallas kernels  16.2 us (24%)
  local copies, waits for them, and re-layouts  0.92 us (1%)
    pallas_call x9, Pallas kernels, call(): pl.pallas_call(kernel, in_specs=[spec(SMEM)] * table + [spec(VMEM)] * (le...  16.2 us
    ppermute x9, waiting for transfers between devices, row_flip(): return lax.ppermute(value, 'row', [(i, i ^ flip) for i in range(8)])  14.2 us
    ppermute x4, waiting for transfers between devices, z_step(): lax.ppermute(value, 'col', [(i, (i + (4 * by if i % 2 == 0 else -4 * by))...  12 us
    ppermute x9, starting transfers between devices, row_flip(): return lax.ppermute(value, 'row', [(i, i ^ flip) for i in range(8)])  10.2 us
    ppermute x4, starting transfers between devices, z_step(): lax.ppermute(value, 'col', [(i, (i + (4 * by if i % 2 == 0 else -4 * by))...  9.78 us
    ppermute x3, starting transfers between devices, col_flip(): return lax.ppermute(value, 'col', [(i, i ^ flip) for i in range(32)])  3.21 us
  transfers between devices with their start and end apart: 16, of which 9 were waited for; matrix products, arithmetic and copies ran while one was open for 0% of the time, Pallas kernels for 18%

profile of v1, /device:TPU:64, one launch (start us, length us, event | category | flops | bytes accessed | tf_op | source)
XLA Modules:
  0.0 68.2 jit_solution(12530558415539268445)
XLA Ops:
  0.0 0.0 copy-start.2
  0.0 1.7 %pack.1.a = bf16[128,256]{1,0:T(8,128)(2,1)} custom-call(s32[32,64]{1,0:T(8,128)} %mask_ref.3, bf16[128,1024]{1,0:T(8,128)(2,1)} %v_ref.1), custom_call_target="tpu_custom_call" | custom-call | flops 1000 | bytes 1000 | tf_op jit(solution)/shard_map/pack/pallas_call | solution.py:149
  1.7 3.0 %collective-permute-start = (bf16[128,256]{1,0:T(8,128)(2,1)}, bf16[128,256]{1,0:T(8,128)(2,1)S(1)}, u32[]{:S(2)}, u32[]{:S(2)}) collective-permute-start(bf16[128,256]{1,0:T(8,128)(2,1)} %pack.1.a), channel_id=1, source_target_pairs={{0,2},{1,3},{2,0},{3,1},{4,6},{5,7},{6,4},{7,5},{8,10},{9,11},{10,... | collective-permute-start | bytes 196616 | tf_op jit(solution)/shard_map/ppermute | solution.py:26
  4.8 1.6 %collective-permute-start.8 = (bf16[1024,512]{1,0:T(8,128)(2,1)}, bf16[1024,512]{1,0:T(8,128)(2,1)S(1)}, u32[]{:S(2)}, u32[]{:S(2)}) collective-permute-start(bf16[1024,512]{1,0:T(8,128)(2,1)} %own.1), channel_id=1, source_target_pairs={{0,32},{32,0},{64,96},{96,64},{128,160},{160,128},{192,224},{224,1... | collective-permute-start | bytes 3145736 | tf_op jit(solution)/shard_map/ppermute | solution.py:22
  6.3 2.2 %collective-permute-start.9 = (bf16[1024,512]{1,0:T(8,128)(2,1)}, bf16[1024,512]{1,0:T(8,128)(2,1)S(1)}, u32[]{:S(2)}, u32[]{:S(2)}) collective-permute-start(bf16[1024,512]{1,0:T(8,128)(2,1)} %own.1), channel_id=1, source_target_pairs={{0,96},{32,64},{64,32},{96,0},{128,224},{160,192},{192,160},{224,1... | collective-permute-start | bytes 3145736 | tf_op jit(solution)/shard_map/ppermute | solution.py:22
  8.5 0.6 collective-permute-start.7
  9.1 0.0 collective-permute-done.b
  9.1 0.0 copy-start.1
  9.1 0.8 %copy-done.1 = bf16[128,256]{1,0:T(8,128)(2,1)S(1)} copy-done((bf16[128,256]{1,0:T(8,128)(2,1)S(1)}, bf16[128,256]{1,0:T(8,128)(2,1)}, u32[]{:S(2)}) %copy-start.1) | copy-done | bytes 65560
  10.0 0.1 collective-permute-start.1
  10.1 1.3 %collective-permute-done.1.b = bf16[2,128,256]{2,1,0:T(8,128)(2,1)S(1)} collective-permute-done((bf16[2,128,256]{2,1,0:T(8,128)(2,1)S(1)}, bf16[2,128,256]{2,1,0:T(8,128)(2,1)S(1)}, u32[]{:S(2)}, u32[]{:S(2)}) %collective-permute-start.1) | collective-permute-done | bytes 131104 | tf_op jit(solution)/shard_map/ppermute | solution.py:26
  11.4 4.6 %collective-permute-start.3 = (bf16[4,128,256]{2,1,0:T(8,128)(2,1)S(1)}, bf16[4,128,256]{2,1,0:T(8,128)(2,1)S(1)}, u32[]{:S(2)}, u32[]{:S(2)}) collective-permute-start(bf16[4,128,256]{2,1,0:T(8,128)(2,1)S(1)} %quad.1), channel_id=1, source_target_pairs={{0,8},{1,25},{2,10},{3,27},{4,12},{5,29},{6,14},{7,31},{8,16},{9,1... | collective-permute-start | bytes 786440 | tf_op jit(solution)/shard_map/ppermute | solution.py:30
  16.0 1.0 %collective-permute-start.2 = (bf16[4,128,256]{2,1,0:T(8,128)(2,1)S(1)}, bf16[4,128,256]{2,1,0:T(8,128)(2,1)S(1)}, u32[]{:S(2)}, u32[]{:S(2)}) collective-permute-start(bf16[4,128,256]{2,1,0:T(8,128)(2,1)S(1)} %quad.1), channel_id=1, source_target_pairs={{0,4},{1,29},{2,6},{3,31},{4,8},{5,1},{6,10},{7,3},{8,12},{9,5},{1... | collective-permute-start | bytes 786440 | tf_op jit(solution)/shard_map/ppermute | solution.py:30
  17.0 5.6 %collective-permute-done.3.b.r2 = bf16[4,128,256]{2,1,0:T(8,128)(2,1)S(1)} collective-permute-done((bf16[4,128,256]{2,1,0:T(8,128)(2,1)S(1)}, bf16[4,128,256]{2,1,0:T(8,128)(2,1)S(1)}, u32[]{:S(2)}, u32[]{:S(2)}) %collective-permute-start.3) | collective-permute-done | bytes 262176 | tf_op jit(solution)/shard_map/ppermute | solution.py:30
  22.6 2.8 %collective-permute-done.2.a.r1 = bf16[4,128,256]{2,1,0:T(8,128)(2,1)S(1)} collective-permute-done((bf16[4,128,256]{2,1,0:T(8,128)(2,1)S(1)}, bf16[4,128,256]{2,1,0:T(8,128)(2,1)S(1)}, u32[]{:S(2)}, u32[]{:S(2)}) %collective-permute-start.2) | collective-permute-done | bytes 262176 | tf_op jit(solution)/shard_map/ppermute | solution.py:30
  25.5 4.2 %collective-permute-start.5 = (bf16[4,128,256]{2,1,0:T(8,128)(2,1)S(1)}, bf16[4,128,256]{2,1,0:T(8,128)(2,1)S(1)}, u32[]{:S(2)}, u32[]{:S(2)}) collective-permute-start(bf16[4,128,256]{2,1,0:T(8,128)(2,1)S(1)} %collective-permute-done.3.b.r2), channel_id=1, source_target_pairs={{0,8},{1,25},{2,10},{3,27},{4,12},{5,29},{6,14},{7,31},{8,16},{9,1... | collective-permute-start | bytes 786440 | tf_op jit(solution)/shard_map/ppermute | solution.py:30
  29.7 0.0 collective-permute-start.4
  29.7 3.1 %collective-permute-done.7.p1 = bf16[1024,512]{1,0:T(8,128)(2,1)S(1)} collective-permute-done((bf16[1024,512]{1,0:T(8,128)(2,1)}, bf16[1024,512]{1,0:T(8,128)(2,1)S(1)}, u32[]{:S(2)}, u32[]{:S(2)}) %collective-permute-start.7) | collective-permute-done | bytes 1048608 | tf_op jit(solution)/shard_map/ppermute | solution.py:22
  32.8 0.0 collective-permute-done.8.q1
  32.8 0.0 collective-permute-done.9.w1
  32.8 0.7 collective-permute-start.11
  33.5 0.9 %collective-permute-start.12 = (bf16[1024,512]{1,0:T(8,128)(2,1)S(1)}, bf16[1024,512]{1,0:T(8,128)(2,1)S(1)}, u32[]{:S(2)}, u32[]{:S(2)}) collective-permute-start(bf16[1024,512]{1,0:T(8,128)(2,1)S(1)} %collective-permute-done.8.q1), channel_id=1, source_target_pairs={{0,96},{32,64},{64,32},{96,0},{128,224},{160,192},{192,160},{224,1... | collective-permute-start | bytes 3145736 | tf_op jit(solution)/shard_map/ppermute | solution.py:22
  34.4 1.1 %collective-permute-start.10 = (bf16[1024,512]{1,0:T(8,128)(2,1)S(1)}, bf16[1024,512]{1,0:T(8,128)(2,1)S(1)}, u32[]{:S(2)}, u32[]{:S(2)}) collective-permute-start(bf16[1024,512]{1,0:T(8,128)(2,1)S(1)} %collective-permute-done.9.w1), channel_id=1, source_target_pairs={{0,128},{32,160},{64,192},{96,224},{128,0},{160,32},{192,64},{224,... | collective-permute-start | bytes 3145736 | tf_op jit(solution)/shard_map/ppermute | solution.py:22
  35.5 0.2 collective-permute-done.5.r4
  35.6 3.5 %collective-permute-done.4.c.r3 = bf16[4,128,256]{2,1,0:T(8,128)(2,1)S(1)} collective-permute-done((bf16[4,128,256]{2,1,0:T(8,128)(2,1)S(1)}, bf16[4,128,256]{2,1,0:T(8,128)(2,1)S(1)}, u32[]{:S(2)}, u32[]{:S(2)}) %collective-permute-start.4) | collective-permute-done | bytes 262176 | tf_op jit(solution)/shard_map/ppermute | solution.py:30
  39.1 0.1 three.1
  39.1 0.1 collective-permute-start.6
  39.2 0.0 copy-done.2
  39.3 2.5 %table.1.table_ref = s32[2,32]{1,0:T(2,128)S(1)} custom-call(s32[32,64]{1,0:T(8,128)S(1)} %copy-done.2), custom_call_target="tpu_custom_call" | custom-call | flops 1000 | bytes 1000 | tf_op jit(solution)/shard_map/table/pallas_call | solution.py:149
  41.7 0.0 copy-start
  41.8 0.0 collective-permute-done.6.theirs
  41.8 1.7 %dense.1.dense_ref = bf16[4096,1024]{1,0:T(8,128)(2,1)S(1)} custom-call(s32[2,32]{1,0:T(2,128)S(1)} %table.1.table_ref, bf16[4,128,256]{2,1,0:T(8,128)(2,1)S(1)} %quad.1, bf16[4,128,256]{2,1,0:T(8,128)(2,1)S(1)} %collective-permute-done.2.a.r1, bf16[4,128,256]{2,1,0:T(8,128)(2,1)S(1)} %collective-permute-done.3.b.r2, ...), custom_call_target="tpu_custom_call" | custom-call | flops 2000000000 | bytes 1000 | tf_op jit(solution)/shard_map/dense/pallas_call | solution.py:149
  43.5 0.0 copy-done
  43.5 4.5 %first.1.acc_in = f32[1024,1024]{1,0:T(8,128)S(1)} custom-call(bf16[4096,1024]{1,0:T(8,128)(2,1)S(1)} %dense.1.dense_ref, bf16[1024,512]{1,0:T(8,128)(2,1)S(1)} %copy-done, bf16[1024,512]{1,0:T(8,128)(2,1)S(1)} %collective-permute-done.7.p1, bf16[1024,512]{1,0:T(8,128)(2,1)S(1)} %collective-permute-done.8.q1, bf16[1024,512]{1,0:T(8,128)(2,1)S(1)} %collective-permute-done.9.w1), custom_call_target="tpu_custom_call" | custom-call | flops 1000 | bytes 1000 | tf_op jit(solution)/shard_map/first/pallas_call | solution.py:149
  48.0 7.9 %collective-permute-done.11.qp = bf16[1024,512]{1,0:T(8,128)(2,1)S(1)} collective-permute-done((bf16[1024,512]{1,0:T(8,128)(2,1)S(1)}, bf16[1024,512]{1,0:T(8,128)(2,1)S(1)}, u32[]{:S(2)}, u32[]{:S(2)}) %collective-permute-start.11) | collective-permute-done | bytes 1048608 | tf_op jit(solution)/shard_map/ppermute | solution.py:22
  56.0 1.8 %collective-permute-start.15 = (bf16[368,512]{1,0:T(8,128)(2,1)S(1)}, bf16[368,512]{1,0:T(8,128)(2,1)S(1)}, u32[]{:S(2)}, u32[]{:S(2)}) collective-permute-start(bf16[368,512]{1,0:T(8,128)(2,1)S(1)} %slice.11), channel_id=1, source_target_pairs={{0,96},{32,64},{64,32},{96,0},{128,224},{160,192},{192,160},{224,1... | collective-permute-start | bytes 1130504 | tf_op jit(solution)/shard_map/ppermute | solution.py:22
  57.8 0.2 collective-permute-done.12.wq
  58.1 0.9 %collective-permute-start.13 = (bf16[352,512]{1,0:T(8,128)(2,1)S(1)}, bf16[352,512]{1,0:T(8,128)(2,1)S(1)}, u32[]{:S(2)}, u32[]{:S(2)}) collective-permute-start(bf16[352,512]{1,0:T(8,128)(2,1)S(1)} %slice.9), channel_id=1, source_target_pairs={{0,128},{32,160},{64,192},{96,224},{128,0},{160,32},{192,64},{224,... | collective-permute-start | bytes 1081352 | tf_op jit(solution)/shard_map/ppermute | solution.py:22
  58.9 0.0 collective-permute-done.10.pw
  58.9 0.5 collective-permute-start.14
  59.4 3.5 %second.1.acc_ref = f32[1024,1024]{1,0:T(8,128)S(1)} custom-call(bf16[4096,1024]{1,0:T(8,128)(2,1)S(1)} %dense.1.dense_ref, f32[1024,1024]{1,0:T(8,128)S(1)} %first.1.acc_in, bf16[1024,512]{1,0:T(8,128)(2,1)S(1)} %collective-permute-done.10.pw, bf16[1024,512]{1,0:T(8,128)(2,1)S(1)} %collective-permute-done.11.qp, ...), custom_call_target="tpu_custom_call", output_to_operand_aliasing={{}: (1, {})} | custom-call | flops 1000 | bytes 1000 | tf_op jit(solution)/shard_map/second/pallas_call | solution.py:149
  63.0 3.0 %collective-permute-done.14.tb = bf16[304,512]{1,0:T(8,128)(2,1)S(1)} collective-permute-done((bf16[304,512]{1,0:T(8,128)(2,1)S(1)}, bf16[304,512]{1,0:T(8,128)(2,1)S(1)}, u32[]{:S(2)}, u32[]{:S(2)}) %collective-permute-start.14) | collective-permute-done | bytes 311328 | tf_op jit(solution)/shard_map/ppermute | solution.py:22
  65.9 0.0 collective-permute-done.13.ta
  65.9 0.0 collective-permute-done.15.tc
  65.9 2.1 %third.1 = bf16[1024,1024]{1,0:T(8,128)(2,1)} custom-call(bf16[4096,1024]{1,0:T(8,128)(2,1)S(1)} %dense.1.dense_ref, f32[1024,1024]{1,0:T(8,128)S(1)} %second.1.acc_ref, bf16[352,512]{1,0:T(8,128)(2,1)S(1)} %collective-permute-done.13.ta, bf16[304,512]{1,0:T(8,128)(2,1)S(1)} %collective-permute-done.14.tb, bf16[368,512]{1,0:T(8,128)(2,1)S(1)} %collective-permute-done.15.tc), custom_call_target="tpu_custom_call" | custom-call | flops 1000 | bytes 1000 | tf_op jit(solution)/shard_map/third/pallas_call | solution.py:149
  (5 shorter events, 0.1 us)
Async XLA Ops:
  0.0 39.3 %copy-start.2 = (s32[32,64]{1,0:T(8,128)S(1)}, s32[32,64]{1,0:T(8,128)}, u32[]{:S(2)}) copy-start(s32[32,64]{1,0:T(8,128)} %mask_ref.3) | copy-start | bytes 24580
  1.7 7.4 %collective-permute-start = (bf16[128,256]{1,0:T(8,128)(2,1)}, bf16[128,256]{1,0:T(8,128)(2,1)S(1)}, u32[]{:S(2)}, u32[]{:S(2)}) collective-permute-start(bf16[128,256]{1,0:T(8,128)(2,1)} %pack.1.a), channel_id=1, source_target_pairs={{0,2},{1,3},{2,0},{3,1},{4,6},{5,7},{6,4},{7,5},{8,10},{9,11},{10,... | collective-permute-start | bytes 196616 | tf_op jit(solution)/shard_map/ppermute | solution.py:26
  4.8 28.0 %collective-permute-start.8 = (bf16[1024,512]{1,0:T(8,128)(2,1)}, bf16[1024,512]{1,0:T(8,128)(2,1)S(1)}, u32[]{:S(2)}, u32[]{:S(2)}) collective-permute-start(bf16[1024,512]{1,0:T(8,128)(2,1)} %own.1), channel_id=1, source_target_pairs={{0,32},{32,0},{64,96},{96,64},{128,160},{160,128},{192,224},{224,1... | collective-permute-start | bytes 3145736 | tf_op jit(solution)/shard_map/ppermute | solution.py:22
  6.3 26.5 %collective-permute-start.9 = (bf16[1024,512]{1,0:T(8,128)(2,1)}, bf16[1024,512]{1,0:T(8,128)(2,1)S(1)}, u32[]{:S(2)}, u32[]{:S(2)}) collective-permute-start(bf16[1024,512]{1,0:T(8,128)(2,1)} %own.1), channel_id=1, source_target_pairs={{0,96},{32,64},{64,32},{96,0},{128,224},{160,192},{192,160},{224,1... | collective-permute-start | bytes 3145736 | tf_op jit(solution)/shard_map/ppermute | solution.py:22
  8.5 24.3 %collective-permute-start.7 = (bf16[1024,512]{1,0:T(8,128)(2,1)}, bf16[1024,512]{1,0:T(8,128)(2,1)S(1)}, u32[]{:S(2)}, u32[]{:S(2)}) collective-permute-start(bf16[1024,512]{1,0:T(8,128)(2,1)} %own.1), channel_id=1, source_target_pairs={{0,128},{32,160},{64,192},{96,224},{128,0},{160,32},{192,64},{224,... | collective-permute-start | bytes 3145736 | tf_op jit(solution)/shard_map/ppermute | solution.py:22
  9.1 0.8 %copy-start.1 = (bf16[128,256]{1,0:T(8,128)(2,1)S(1)}, bf16[128,256]{1,0:T(8,128)(2,1)}, u32[]{:S(2)}) copy-start(bf16[128,256]{1,0:T(8,128)(2,1)} %pack.1.a) | copy-start | bytes 196612
  10.0 1.4 %collective-permute-start.1 = (bf16[2,128,256]{2,1,0:T(8,128)(2,1)S(1)}, bf16[2,128,256]{2,1,0:T(8,128)(2,1)S(1)}, u32[]{:S(2)}, u32[]{:S(2)}) collective-permute-start(bf16[2,128,256]{2,1,0:T(8,128)(2,1)S(1)} %pair.1.a), channel_id=1, source_target_pairs={{0,1},{1,0},{2,3},{3,2},{4,5},{5,4},{6,7},{7,6},{8,9},{9,8},{10,11... | collective-permute-start | bytes 393224 | tf_op jit(solution)/shard_map/ppermute | solution.py:26
  11.4 11.2 %collective-permute-start.3 = (bf16[4,128,256]{2,1,0:T(8,128)(2,1)S(1)}, bf16[4,128,256]{2,1,0:T(8,128)(2,1)S(1)}, u32[]{:S(2)}, u32[]{:S(2)}) collective-permute-start(bf16[4,128,256]{2,1,0:T(8,128)(2,1)S(1)} %quad.1), channel_id=1, source_target_pairs={{0,8},{1,25},{2,10},{3,27},{4,12},{5,29},{6,14},{7,31},{8,16},{9,1... | collective-permute-start | bytes 786440 | tf_op jit(solution)/shard_map/ppermute | solution.py:30
  16.0 9.5 %collective-permute-start.2 = (bf16[4,128,256]{2,1,0:T(8,128)(2,1)S(1)}, bf16[4,128,256]{2,1,0:T(8,128)(2,1)S(1)}, u32[]{:S(2)}, u32[]{:S(2)}) collective-permute-start(bf16[4,128,256]{2,1,0:T(8,128)(2,1)S(1)} %quad.1), channel_id=1, source_target_pairs={{0,4},{1,29},{2,6},{3,31},{4,8},{5,1},{6,10},{7,3},{8,12},{9,5},{1... | collective-permute-start | bytes 786440 | tf_op jit(solution)/shard_map/ppermute | solution.py:30
  25.5 10.2 %collective-permute-start.5 = (bf16[4,128,256]{2,1,0:T(8,128)(2,1)S(1)}, bf16[4,128,256]{2,1,0:T(8,128)(2,1)S(1)}, u32[]{:S(2)}, u32[]{:S(2)}) collective-permute-start(bf16[4,128,256]{2,1,0:T(8,128)(2,1)S(1)} %collective-permute-done.3.b.r2), channel_id=1, source_target_pairs={{0,8},{1,25},{2,10},{3,27},{4,12},{5,29},{6,14},{7,31},{8,16},{9,1... | collective-permute-start | bytes 786440 | tf_op jit(solution)/shard_map/ppermute | solution.py:30
  29.7 9.4 %collective-permute-start.4 = (bf16[4,128,256]{2,1,0:T(8,128)(2,1)S(1)}, bf16[4,128,256]{2,1,0:T(8,128)(2,1)S(1)}, u32[]{:S(2)}, u32[]{:S(2)}) collective-permute-start(bf16[4,128,256]{2,1,0:T(8,128)(2,1)S(1)} %collective-permute-done.3.b.r2), channel_id=1, source_target_pairs={{0,4},{1,29},{2,6},{3,31},{4,8},{5,1},{6,10},{7,3},{8,12},{9,5},{1... | collective-permute-start | bytes 786440 | tf_op jit(solution)/shard_map/ppermute | solution.py:30
  32.8 23.1 %collective-permute-start.11 = (bf16[1024,512]{1,0:T(8,128)(2,1)S(1)}, bf16[1024,512]{1,0:T(8,128)(2,1)S(1)}, u32[]{:S(2)}, u32[]{:S(2)}) collective-permute-start(bf16[1024,512]{1,0:T(8,128)(2,1)S(1)} %collective-permute-done.7.p1), channel_id=1, source_target_pairs={{0,32},{32,0},{64,96},{96,64},{128,160},{160,128},{192,224},{224,1... | collective-permute-start | bytes 3145736 | tf_op jit(solution)/shard_map/ppermute | solution.py:22
  33.5 24.5 %collective-permute-start.12 = (bf16[1024,512]{1,0:T(8,128)(2,1)S(1)}, bf16[1024,512]{1,0:T(8,128)(2,1)S(1)}, u32[]{:S(2)}, u32[]{:S(2)}) collective-permute-start(bf16[1024,512]{1,0:T(8,128)(2,1)S(1)} %collective-permute-done.8.q1), channel_id=1, source_target_pairs={{0,96},{32,64},{64,32},{96,0},{128,224},{160,192},{192,160},{224,1... | collective-permute-start | bytes 3145736 | tf_op jit(solution)/shard_map/ppermute | solution.py:22
  34.4 24.5 %collective-permute-start.10 = (bf16[1024,512]{1,0:T(8,128)(2,1)S(1)}, bf16[1024,512]{1,0:T(8,128)(2,1)S(1)}, u32[]{:S(2)}, u32[]{:S(2)}) collective-permute-start(bf16[1024,512]{1,0:T(8,128)(2,1)S(1)} %collective-permute-done.9.w1), channel_id=1, source_target_pairs={{0,128},{32,160},{64,192},{96,224},{128,0},{160,32},{192,64},{224,... | collective-permute-start | bytes 3145736 | tf_op jit(solution)/shard_map/ppermute | solution.py:22
  39.1 2.6 %collective-permute-start.6 = (bf16[12,128,256]{2,1,0:T(8,128)(2,1)S(1)}, bf16[12,128,256]{2,1,0:T(8,128)(2,1)S(1)}, u32[]{:S(2)}, u32[]{:S(2)}) collective-permute-start(bf16[12,128,256]{2,1,0:T(8,128)(2,1)S(1)} %three.1), channel_id=1, source_target_pairs={{0,1},{1,0},{2,3},{3,2},{4,5},{5,4},{6,7},{7,6},{8,9},{9,8},{10,11... | collective-permute-start | bytes 2359304 | tf_op jit(solution)/shard_map/ppermute | solution.py:26
  41.7 1.8 %copy-start = (bf16[1024,512]{1,0:T(8,128)(2,1)S(1)}, bf16[1024,512]{1,0:T(8,128)(2,1)}, u32[]{:S(2)}) copy-start(bf16[1024,512]{1,0:T(8,128)(2,1)} %own.1) | copy-start | bytes 3145732
  56.0 10.0 %collective-permute-start.15 = (bf16[368,512]{1,0:T(8,128)(2,1)S(1)}, bf16[368,512]{1,0:T(8,128)(2,1)S(1)}, u32[]{:S(2)}, u32[]{:S(2)}) collective-permute-start(bf16[368,512]{1,0:T(8,128)(2,1)S(1)} %slice.11), channel_id=1, source_target_pairs={{0,96},{32,64},{64,32},{96,0},{128,224},{160,192},{192,160},{224,1... | collective-permute-start | bytes 1130504 | tf_op jit(solution)/shard_map/ppermute | solution.py:22
  58.1 7.9 %collective-permute-start.13 = (bf16[352,512]{1,0:T(8,128)(2,1)S(1)}, bf16[352,512]{1,0:T(8,128)(2,1)S(1)}, u32[]{:S(2)}, u32[]{:S(2)}) collective-permute-start(bf16[352,512]{1,0:T(8,128)(2,1)S(1)} %slice.9), channel_id=1, source_target_pairs={{0,128},{32,160},{64,192},{96,224},{128,0},{160,32},{192,64},{224,... | collective-permute-start | bytes 1081352 | tf_op jit(solution)/shard_map/ppermute | solution.py:22
  58.9 7.0 %collective-permute-start.14 = (bf16[304,512]{1,0:T(8,128)(2,1)S(1)}, bf16[304,512]{1,0:T(8,128)(2,1)S(1)}, u32[]{:S(2)}, u32[]{:S(2)}) collective-permute-start(bf16[304,512]{1,0:T(8,128)(2,1)S(1)} %slice.10), channel_id=1, source_target_pairs={{0,32},{32,0},{64,96},{96,64},{128,160},{160,128},{192,224},{224,1... | collective-permute-start | bytes 933896 | tf_op jit(solution)/shard_map/ppermute | solution.py:22

commit v2 on v1

--- a/solution.py
+++ b/solution.py
@@ -170,14 +170,14 @@
     pair = call(join_kernel, (packed, col_flip(packed, 2)), (2, TILE, 2 * TILE), BF16, "pair", flops=20000000000)
     quad = call(join_kernel, (pair, col_flip(pair, 1)), (4, TILE, 2 * TILE), BF16, "quad")
     r1, r2 = barrier((z_step(quad, 1), z_step(quad, 2)))
-    p1, q1, w1 = barrier((p1, q1, w1))
+
     r3, r4 = barrier((z_step(r2, 1), z_step(r2, 2)))
     theirs = col_flip(call(three_kernel, (r1, r2, r3), (12, TILE, 2 * TILE), BF16, "three"), 1)
     dense = call(
         dense_kernel, (table, quad, r1, r2, r3, r4, theirs), (4096, 1024), BF16, "dense", table=True, flops=2000000000
     )
 
-    pw, qp, wq = row_flip(w1, 4), row_flip(p1, 1), row_flip(q1, 3)
+    pw, qp, wq = row_flip(p1, 3), row_flip(q1, 4), row_flip(w1, 1)
     acc = call(first_kernel, (dense, amps, p1, q1, w1), (1024, 1024), jnp.float32, "first")
     wq, pw, qp = (barrier((acc, v))[1] for v in (wq, pw, qp))
     a, b, _ = PARTS

time: 68.3 us -> 69.1 us (1.012)
  waiting for transfers between devices: 27.6 us -> 28.6 us
    ppermute x4, waiting for transfers between devices: 12 us -> 13.2 us  [z_step(): lax.ppermute(value, 'col', [(i, (i + (4 * by if i % 2 == 0 else -4 * by))...]
  transfers between devices with their start and end apart: 16 -> 16, of which waited for: 9 -> 10; matrix products, arithmetic and copies ran while one was open for 0% -> 0% of each run, Pallas kernels for 18% -> 18%
where the time goes in v2:
time: 69.1 us; the launch traced here: 68.9 us
  waiting for transfers between devices  28.6 us (41%)
  starting transfers between devices  22.9 us (33%)
  Pallas kernels  16.2 us (23%)
  local copies, waits for them, and re-layouts  0.92 us (1%)
    pallas_call x9, Pallas kernels, call(): pl.pallas_call(kernel, in_specs=[spec(SMEM)] * table + [spec(VMEM)] * (le...  16.2 us
    ppermute x9, waiting for transfers between devices, row_flip(): return lax.ppermute(value, 'row', [(i, i ^ flip) for i in range(8)])  14.1 us
    ppermute x4, waiting for transfers between devices, z_step(): lax.ppermute(value, 'col', [(i, (i + (4 * by if i % 2 == 0 else -4 * by))...  13.2 us
    ppermute x9, starting transfers between devices, row_flip(): return lax.ppermute(value, 'row', [(i, i ^ flip) for i in range(8)])  9.94 us
    ppermute x4, starting transfers between devices, z_step(): lax.ppermute(value, 'col', [(i, (i + (4 * by if i % 2 == 0 else -4 * by))...  9.78 us
    ppermute x3, starting transfers between devices, col_flip(): return lax.ppermute(value, 'col', [(i, i ^ flip) for i in range(32)])  3.21 us
  transfers between devices with their start and end apart: 16, of which 10 were waited for; matrix products, arithmetic and copies ran while one was open for 0% of the time, Pallas kernels for 18%

profile of v2, /device:TPU:64, one launch (start us, length us, event | category | flops | bytes accessed | tf_op | source)
XLA Modules:
  0.0 68.9 jit_solution(17472042987295072060)
XLA Ops:
  0.0 0.0 copy-start.2
  0.0 1.7 %pack.1.a = bf16[128,256]{1,0:T(8,128)(2,1)} custom-call(s32[32,64]{1,0:T(8,128)} %mask_ref.3, bf16[128,1024]{1,0:T(8,128)(2,1)} %v_ref.1), custom_call_target="tpu_custom_call" | custom-call | flops 1000 | bytes 1000 | tf_op jit(solution)/shard_map/pack/pallas_call | solution.py:149
  1.7 3.0 %collective-permute-start = (bf16[128,256]{1,0:T(8,128)(2,1)}, bf16[128,256]{1,0:T(8,128)(2,1)S(1)}, u32[]{:S(2)}, u32[]{:S(2)}) collective-permute-start(bf16[128,256]{1,0:T(8,128)(2,1)} %pack.1.a), channel_id=1, source_target_pairs={{0,2},{1,3},{2,0},{3,1},{4,6},{5,7},{6,4},{7,5},{8,10},{9,11},{10,... | collective-permute-start | bytes 196616 | tf_op jit(solution)/shard_map/ppermute | solution.py:26
  4.8 1.6 %collective-permute-start.8 = (bf16[1024,512]{1,0:T(8,128)(2,1)}, bf16[1024,512]{1,0:T(8,128)(2,1)S(1)}, u32[]{:S(2)}, u32[]{:S(2)}) collective-permute-start(bf16[1024,512]{1,0:T(8,128)(2,1)} %own.1), channel_id=1, source_target_pairs={{0,32},{32,0},{64,96},{96,64},{128,160},{160,128},{192,224},{224,1... | collective-permute-start | bytes 3145736 | tf_op jit(solution)/shard_map/ppermute | solution.py:22
  6.3 2.2 %collective-permute-start.9 = (bf16[1024,512]{1,0:T(8,128)(2,1)}, bf16[1024,512]{1,0:T(8,128)(2,1)S(1)}, u32[]{:S(2)}, u32[]{:S(2)}) collective-permute-start(bf16[1024,512]{1,0:T(8,128)(2,1)} %own.1), channel_id=1, source_target_pairs={{0,96},{32,64},{64,32},{96,0},{128,224},{160,192},{192,160},{224,1... | collective-permute-start | bytes 3145736 | tf_op jit(solution)/shard_map/ppermute | solution.py:22
  8.5 0.6 collective-permute-start.7
  9.1 0.0 collective-permute-done.b
  9.1 0.0 copy-start.1
  9.1 0.8 %copy-done.1 = bf16[128,256]{1,0:T(8,128)(2,1)S(1)} copy-done((bf16[128,256]{1,0:T(8,128)(2,1)S(1)}, bf16[128,256]{1,0:T(8,128)(2,1)}, u32[]{:S(2)}) %copy-start.1) | copy-done | bytes 65560
  10.0 0.1 collective-permute-start.1
  10.1 1.3 %collective-permute-done.1.b = bf16[2,128,256]{2,1,0:T(8,128)(2,1)S(1)} collective-permute-done((bf16[2,128,256]{2,1,0:T(8,128)(2,1)S(1)}, bf16[2,128,256]{2,1,0:T(8,128)(2,1)S(1)}, u32[]{:S(2)}, u32[]{:S(2)}) %collective-permute-start.1) | collective-permute-done | bytes 131104 | tf_op jit(solution)/shard_map/ppermute | solution.py:26
  11.4 4.6 %collective-permute-start.3 = (bf16[4,128,256]{2,1,0:T(8,128)(2,1)S(1)}, bf16[4,128,256]{2,1,0:T(8,128)(2,1)S(1)}, u32[]{:S(2)}, u32[]{:S(2)}) collective-permute-start(bf16[4,128,256]{2,1,0:T(8,128)(2,1)S(1)} %quad.1), channel_id=1, source_target_pairs={{0,8},{1,25},{2,10},{3,27},{4,12},{5,29},{6,14},{7,31},{8,16},{9,1... | collective-permute-start | bytes 786440 | tf_op jit(solution)/shard_map/ppermute | solution.py:30
  16.0 1.0 %collective-permute-start.2 = (bf16[4,128,256]{2,1,0:T(8,128)(2,1)S(1)}, bf16[4,128,256]{2,1,0:T(8,128)(2,1)S(1)}, u32[]{:S(2)}, u32[]{:S(2)}) collective-permute-start(bf16[4,128,256]{2,1,0:T(8,128)(2,1)S(1)} %quad.1), channel_id=1, source_target_pairs={{0,4},{1,29},{2,6},{3,31},{4,8},{5,1},{6,10},{7,3},{8,12},{9,5},{1... | collective-permute-start | bytes 786440 | tf_op jit(solution)/shard_map/ppermute | solution.py:30
  17.0 5.6 %collective-permute-done.3.b.r2 = bf16[4,128,256]{2,1,0:T(8,128)(2,1)S(1)} collective-permute-done((bf16[4,128,256]{2,1,0:T(8,128)(2,1)S(1)}, bf16[4,128,256]{2,1,0:T(8,128)(2,1)S(1)}, u32[]{:S(2)}, u32[]{:S(2)}) %collective-permute-start.3) | collective-permute-done | bytes 262176 | tf_op jit(solution)/shard_map/ppermute | solution.py:30
  22.6 2.8 %collective-permute-done.2.a.r1 = bf16[4,128,256]{2,1,0:T(8,128)(2,1)S(1)} collective-permute-done((bf16[4,128,256]{2,1,0:T(8,128)(2,1)S(1)}, bf16[4,128,256]{2,1,0:T(8,128)(2,1)S(1)}, u32[]{:S(2)}, u32[]{:S(2)}) %collective-permute-start.2) | collective-permute-done | bytes 262176 | tf_op jit(solution)/shard_map/ppermute | solution.py:30
  25.5 4.2 %collective-permute-start.5 = (bf16[4,128,256]{2,1,0:T(8,128)(2,1)S(1)}, bf16[4,128,256]{2,1,0:T(8,128)(2,1)S(1)}, u32[]{:S(2)}, u32[]{:S(2)}) collective-permute-start(bf16[4,128,256]{2,1,0:T(8,128)(2,1)S(1)} %collective-permute-done.3.b.r2), channel_id=1, source_target_pairs={{0,8},{1,25},{2,10},{3,27},{4,12},{5,29},{6,14},{7,31},{8,16},{9,1... | collective-permute-start | bytes 786440 | tf_op jit(solution)/shard_map/ppermute | solution.py:30
  29.7 0.0 collective-permute-start.4
  29.7 0.0 collective-permute-done.8.q1
  29.7 1.4 %collective-permute-start.11 = (bf16[1024,512]{1,0:T(8,128)(2,1)S(1)}, bf16[1024,512]{1,0:T(8,128)(2,1)S(1)}, u32[]{:S(2)}, u32[]{:S(2)}) collective-permute-start(bf16[1024,512]{1,0:T(8,128)(2,1)S(1)} %collective-permute-done.8.q1), channel_id=1, source_target_pairs={{0,128},{32,160},{64,192},{96,224},{128,0},{160,32},{192,64},{224,... | collective-permute-start | bytes 3145736 | tf_op jit(solution)/shard_map/ppermute | solution.py:22
  31.1 1.0 %collective-permute-done.9.w1 = bf16[1024,512]{1,0:T(8,128)(2,1)S(1)} collective-permute-done((bf16[1024,512]{1,0:T(8,128)(2,1)}, bf16[1024,512]{1,0:T(8,128)(2,1)S(1)}, u32[]{:S(2)}, u32[]{:S(2)}) %collective-permute-start.9) | collective-permute-done | bytes 1048608 | tf_op jit(solution)/shard_map/ppermute | solution.py:22
  32.1 0.0 collective-permute-start.12
  32.1 1.4 %collective-permute-done.7.p1 = bf16[1024,512]{1,0:T(8,128)(2,1)S(1)} collective-permute-done((bf16[1024,512]{1,0:T(8,128)(2,1)}, bf16[1024,512]{1,0:T(8,128)(2,1)S(1)}, u32[]{:S(2)}, u32[]{:S(2)}) %collective-permute-start.7) | collective-permute-done | bytes 1048608 | tf_op jit(solution)/shard_map/ppermute | solution.py:22
  33.5 0.8 %collective-permute-start.10 = (bf16[1024,512]{1,0:T(8,128)(2,1)S(1)}, bf16[1024,512]{1,0:T(8,128)(2,1)S(1)}, u32[]{:S(2)}, u32[]{:S(2)}) collective-permute-start(bf16[1024,512]{1,0:T(8,128)(2,1)S(1)} %collective-permute-done.7.p1), channel_id=1, source_target_pairs={{0,96},{32,64},{64,32},{96,0},{128,224},{160,192},{192,160},{224,1... | collective-permute-start | bytes 3145736 | tf_op jit(solution)/shard_map/ppermute | solution.py:22
  34.4 1.3 %collective-permute-done.5.r4 = bf16[4,128,256]{2,1,0:T(8,128)(2,1)S(1)} collective-permute-done((bf16[4,128,256]{2,1,0:T(8,128)(2,1)S(1)}, bf16[4,128,256]{2,1,0:T(8,128)(2,1)S(1)}, u32[]{:S(2)}, u32[]{:S(2)}) %collective-permute-start.5) | collective-permute-done | bytes 262176 | tf_op jit(solution)/shard_map/ppermute | solution.py:30
  35.6 3.5 %collective-permute-done.4.c.r3 = bf16[4,128,256]{2,1,0:T(8,128)(2,1)S(1)} collective-permute-done((bf16[4,128,256]{2,1,0:T(8,128)(2,1)S(1)}, bf16[4,128,256]{2,1,0:T(8,128)(2,1)S(1)}, u32[]{:S(2)}, u32[]{:S(2)}) %collective-permute-start.4) | collective-permute-done | bytes 262176 | tf_op jit(solution)/shard_map/ppermute | solution.py:30
  39.1 0.1 three.1
  39.1 0.1 collective-permute-start.6
  39.2 0.0 copy-done.2
  39.3 2.5 %table.1.table_ref = s32[2,32]{1,0:T(2,128)S(1)} custom-call(s32[32,64]{1,0:T(8,128)S(1)} %copy-done.2), custom_call_target="tpu_custom_call" | custom-call | flops 1000 | bytes 1000 | tf_op jit(solution)/shard_map/table/pallas_call | solution.py:149
  41.7 0.0 copy-start
  41.8 0.0 collective-permute-done.6.theirs
  41.8 1.7 %dense.1.dense_ref = bf16[4096,1024]{1,0:T(8,128)(2,1)S(1)} custom-call(s32[2,32]{1,0:T(2,128)S(1)} %table.1.table_ref, bf16[4,128,256]{2,1,0:T(8,128)(2,1)S(1)} %quad.1, bf16[4,128,256]{2,1,0:T(8,128)(2,1)S(1)} %collective-permute-done.2.a.r1, bf16[4,128,256]{2,1,0:T(8,128)(2,1)S(1)} %collective-permute-done.3.b.r2, ...), custom_call_target="tpu_custom_call" | custom-call | flops 2000000000 | bytes 1000 | tf_op jit(solution)/shard_map/dense/pallas_call | solution.py:149
  43.5 0.0 copy-done
  43.5 4.5 %first.1.acc_in = f32[1024,1024]{1,0:T(8,128)S(1)} custom-call(bf16[4096,1024]{1,0:T(8,128)(2,1)S(1)} %dense.1.dense_ref, bf16[1024,512]{1,0:T(8,128)(2,1)S(1)} %copy-done, bf16[1024,512]{1,0:T(8,128)(2,1)S(1)} %collective-permute-done.7.p1, bf16[1024,512]{1,0:T(8,128)(2,1)S(1)} %collective-permute-done.8.q1, bf16[1024,512]{1,0:T(8,128)(2,1)S(1)} %collective-permute-done.9.w1), custom_call_target="tpu_custom_call" | custom-call | flops 1000 | bytes 1000 | tf_op jit(solution)/shard_map/first/pallas_call | solution.py:149
  48.0 7.2 %collective-permute-done.11.qp = bf16[1024,512]{1,0:T(8,128)(2,1)S(1)} collective-permute-done((bf16[1024,512]{1,0:T(8,128)(2,1)S(1)}, bf16[1024,512]{1,0:T(8,128)(2,1)S(1)}, u32[]{:S(2)}, u32[]{:S(2)}) %collective-permute-start.11) | collective-permute-done | bytes 1048608 | tf_op jit(solution)/shard_map/ppermute | solution.py:22
  55.3 1.2 %collective-permute-start.15 = (bf16[368,512]{1,0:T(8,128)(2,1)S(1)}, bf16[368,512]{1,0:T(8,128)(2,1)S(1)}, u32[]{:S(2)}, u32[]{:S(2)}) collective-permute-start(bf16[368,512]{1,0:T(8,128)(2,1)S(1)} %slice.11), channel_id=1, source_target_pairs={{0,96},{32,64},{64,32},{96,0},{128,224},{160,192},{192,160},{224,1... | collective-permute-start | bytes 1130504 | tf_op jit(solution)/shard_map/ppermute | solution.py:22
  56.5 0.0 collective-permute-done.12.wq
  56.5 2.0 %collective-permute-start.13 = (bf16[352,512]{1,0:T(8,128)(2,1)S(1)}, bf16[352,512]{1,0:T(8,128)(2,1)S(1)}, u32[]{:S(2)}, u32[]{:S(2)}) collective-permute-start(bf16[352,512]{1,0:T(8,128)(2,1)S(1)} %slice.9), channel_id=1, source_target_pairs={{0,128},{32,160},{64,192},{96,224},{128,0},{160,32},{192,64},{224,... | collective-permute-start | bytes 1081352 | tf_op jit(solution)/shard_map/ppermute | solution.py:22
  58.6 0.0 collective-permute-done.10.pw
  58.6 0.1 collective-permute-start.14
  58.7 3.5 %second.1.acc_ref = f32[1024,1024]{1,0:T(8,128)S(1)} custom-call(bf16[4096,1024]{1,0:T(8,128)(2,1)S(1)} %dense.1.dense_ref, f32[1024,1024]{1,0:T(8,128)S(1)} %first.1.acc_in, bf16[1024,512]{1,0:T(8,128)(2,1)S(1)} %collective-permute-done.10.pw, bf16[1024,512]{1,0:T(8,128)(2,1)S(1)} %collective-permute-done.11.qp, ...), custom_call_target="tpu_custom_call", output_to_operand_aliasing={{}: (1, {})} | custom-call | flops 1000 | bytes 1000 | tf_op jit(solution)/shard_map/second/pallas_call | solution.py:149
  62.2 4.0 %collective-permute-done.14.tb = bf16[304,512]{1,0:T(8,128)(2,1)S(1)} collective-permute-done((bf16[304,512]{1,0:T(8,128)(2,1)S(1)}, bf16[304,512]{1,0:T(8,128)(2,1)S(1)}, u32[]{:S(2)}, u32[]{:S(2)}) %collective-permute-start.14) | collective-permute-done | bytes 311328 | tf_op jit(solution)/shard_map/ppermute | solution.py:22
  66.2 0.0 collective-permute-done.13.ta
  66.2 0.4 collective-permute-done.15.tc
  66.6 2.1 %third.1 = bf16[1024,1024]{1,0:T(8,128)(2,1)} custom-call(bf16[4096,1024]{1,0:T(8,128)(2,1)S(1)} %dense.1.dense_ref, f32[1024,1024]{1,0:T(8,128)S(1)} %second.1.acc_ref, bf16[352,512]{1,0:T(8,128)(2,1)S(1)} %collective-permute-done.13.ta, bf16[304,512]{1,0:T(8,128)(2,1)S(1)} %collective-permute-done.14.tb, bf16[368,512]{1,0:T(8,128)(2,1)S(1)} %collective-permute-done.15.tc), custom_call_target="tpu_custom_call" | custom-call | flops 1000 | bytes 1000 | tf_op jit(solution)/shard_map/third/pallas_call | solution.py:149
  (5 shorter events, 0.1 us)
Async XLA Ops:
  0.0 39.3 %copy-start.2 = (s32[32,64]{1,0:T(8,128)S(1)}, s32[32,64]{1,0:T(8,128)}, u32[]{:S(2)}) copy-start(s32[32,64]{1,0:T(8,128)} %mask_ref.3) | copy-start | bytes 24580
  1.7 7.4 %collective-permute-start = (bf16[128,256]{1,0:T(8,128)(2,1)}, bf16[128,256]{1,0:T(8,128)(2,1)S(1)}, u32[]{:S(2)}, u32[]{:S(2)}) collective-permute-start(bf16[128,256]{1,0:T(8,128)(2,1)} %pack.1.a), channel_id=1, source_target_pairs={{0,2},{1,3},{2,0},{3,1},{4,6},{5,7},{6,4},{7,5},{8,10},{9,11},{10,... | collective-permute-start | bytes 196616 | tf_op jit(solution)/shard_map/ppermute | solution.py:26
  4.8 24.9 %collective-permute-start.8 = (bf16[1024,512]{1,0:T(8,128)(2,1)}, bf16[1024,512]{1,0:T(8,128)(2,1)S(1)}, u32[]{:S(2)}, u32[]{:S(2)}) collective-permute-start(bf16[1024,512]{1,0:T(8,128)(2,1)} %own.1), channel_id=1, source_target_pairs={{0,32},{32,0},{64,96},{96,64},{128,160},{160,128},{192,224},{224,1... | collective-permute-start | bytes 3145736 | tf_op jit(solution)/shard_map/ppermute | solution.py:22
  6.3 25.8 %collective-permute-start.9 = (bf16[1024,512]{1,0:T(8,128)(2,1)}, bf16[1024,512]{1,0:T(8,128)(2,1)S(1)}, u32[]{:S(2)}, u32[]{:S(2)}) collective-permute-start(bf16[1024,512]{1,0:T(8,128)(2,1)} %own.1), channel_id=1, source_target_pairs={{0,96},{32,64},{64,32},{96,0},{128,224},{160,192},{192,160},{224,1... | collective-permute-start | bytes 3145736 | tf_op jit(solution)/shard_map/ppermute | solution.py:22
  8.5 25.0 %collective-permute-start.7 = (bf16[1024,512]{1,0:T(8,128)(2,1)}, bf16[1024,512]{1,0:T(8,128)(2,1)S(1)}, u32[]{:S(2)}, u32[]{:S(2)}) collective-permute-start(bf16[1024,512]{1,0:T(8,128)(2,1)} %own.1), channel_id=1, source_target_pairs={{0,128},{32,160},{64,192},{96,224},{128,0},{160,32},{192,64},{224,... | collective-permute-start | bytes 3145736 | tf_op jit(solution)/shard_map/ppermute | solution.py:22
  9.1 0.8 %copy-start.1 = (bf16[128,256]{1,0:T(8,128)(2,1)S(1)}, bf16[128,256]{1,0:T(8,128)(2,1)}, u32[]{:S(2)}) copy-start(bf16[128,256]{1,0:T(8,128)(2,1)} %pack.1.a) | copy-start | bytes 196612
  10.0 1.4 %collective-permute-start.1 = (bf16[2,128,256]{2,1,0:T(8,128)(2,1)S(1)}, bf16[2,128,256]{2,1,0:T(8,128)(2,1)S(1)}, u32[]{:S(2)}, u32[]{:S(2)}) collective-permute-start(bf16[2,128,256]{2,1,0:T(8,128)(2,1)S(1)} %pair.1.a), channel_id=1, source_target_pairs={{0,1},{1,0},{2,3},{3,2},{4,5},{5,4},{6,7},{7,6},{8,9},{9,8},{10,11... | collective-permute-start | bytes 393224 | tf_op jit(solution)/shard_map/ppermute | solution.py:26
  11.4 11.2 %collective-permute-start.3 = (bf16[4,128,256]{2,1,0:T(8,128)(2,1)S(1)}, bf16[4,128,256]{2,1,0:T(8,128)(2,1)S(1)}, u32[]{:S(2)}, u32[]{:S(2)}) collective-permute-start(bf16[4,128,256]{2,1,0:T(8,128)(2,1)S(1)} %quad.1), channel_id=1, source_target_pairs={{0,8},{1,25},{2,10},{3,27},{4,12},{5,29},{6,14},{7,31},{8,16},{9,1... | collective-permute-start | bytes 786440 | tf_op jit(solution)/shard_map/ppermute | solution.py:30
  16.0 9.5 %collective-permute-start.2 = (bf16[4,128,256]{2,1,0:T(8,128)(2,1)S(1)}, bf16[4,128,256]{2,1,0:T(8,128)(2,1)S(1)}, u32[]{:S(2)}, u32[]{:S(2)}) collective-permute-start(bf16[4,128,256]{2,1,0:T(8,128)(2,1)S(1)} %quad.1), channel_id=1, source_target_pairs={{0,4},{1,29},{2,6},{3,31},{4,8},{5,1},{6,10},{7,3},{8,12},{9,5},{1... | collective-permute-start | bytes 786440 | tf_op jit(solution)/shard_map/ppermute | solution.py:30
  25.5 10.2 %collective-permute-start.5 = (bf16[4,128,256]{2,1,0:T(8,128)(2,1)S(1)}, bf16[4,128,256]{2,1,0:T(8,128)(2,1)S(1)}, u32[]{:S(2)}, u32[]{:S(2)}) collective-permute-start(bf16[4,128,256]{2,1,0:T(8,128)(2,1)S(1)} %collective-permute-done.3.b.r2), channel_id=1, source_target_pairs={{0,8},{1,25},{2,10},{3,27},{4,12},{5,29},{6,14},{7,31},{8,16},{9,1... | collective-permute-start | bytes 786440 | tf_op jit(solution)/shard_map/ppermute | solution.py:30
  29.7 9.4 %collective-permute-start.4 = (bf16[4,128,256]{2,1,0:T(8,128)(2,1)S(1)}, bf16[4,128,256]{2,1,0:T(8,128)(2,1)S(1)}, u32[]{:S(2)}, u32[]{:S(2)}) collective-permute-start(bf16[4,128,256]{2,1,0:T(8,128)(2,1)S(1)} %collective-permute-done.3.b.r2), channel_id=1, source_target_pairs={{0,4},{1,29},{2,6},{3,31},{4,8},{5,1},{6,10},{7,3},{8,12},{9,5},{1... | collective-permute-start | bytes 786440 | tf_op jit(solution)/shard_map/ppermute | solution.py:30
  29.7 25.6 %collective-permute-start.11 = (bf16[1024,512]{1,0:T(8,128)(2,1)S(1)}, bf16[1024,512]{1,0:T(8,128)(2,1)S(1)}, u32[]{:S(2)}, u32[]{:S(2)}) collective-permute-start(bf16[1024,512]{1,0:T(8,128)(2,1)S(1)} %collective-permute-done.8.q1), channel_id=1, source_target_pairs={{0,128},{32,160},{64,192},{96,224},{128,0},{160,32},{192,64},{224,... | collective-permute-start | bytes 3145736 | tf_op jit(solution)/shard_map/ppermute | solution.py:22
  32.1 24.4 %collective-permute-start.12 = (bf16[1024,512]{1,0:T(8,128)(2,1)S(1)}, bf16[1024,512]{1,0:T(8,128)(2,1)S(1)}, u32[]{:S(2)}, u32[]{:S(2)}) collective-permute-start(bf16[1024,512]{1,0:T(8,128)(2,1)S(1)} %collective-permute-done.9.w1), channel_id=1, source_target_pairs={{0,32},{32,0},{64,96},{96,64},{128,160},{160,128},{192,224},{224,1... | collective-permute-start | bytes 3145736 | tf_op jit(solution)/shard_map/ppermute | solution.py:22
  33.5 25.0 %collective-permute-start.10 = (bf16[1024,512]{1,0:T(8,128)(2,1)S(1)}, bf16[1024,512]{1,0:T(8,128)(2,1)S(1)}, u32[]{:S(2)}, u32[]{:S(2)}) collective-permute-start(bf16[1024,512]{1,0:T(8,128)(2,1)S(1)} %collective-permute-done.7.p1), channel_id=1, source_target_pairs={{0,96},{32,64},{64,32},{96,0},{128,224},{160,192},{192,160},{224,1... | collective-permute-start | bytes 3145736 | tf_op jit(solution)/shard_map/ppermute | solution.py:22
  39.1 2.6 %collective-permute-start.6 = (bf16[12,128,256]{2,1,0:T(8,128)(2,1)S(1)}, bf16[12,128,256]{2,1,0:T(8,128)(2,1)S(1)}, u32[]{:S(2)}, u32[]{:S(2)}) collective-permute-start(bf16[12,128,256]{2,1,0:T(8,128)(2,1)S(1)} %three.1), channel_id=1, source_target_pairs={{0,1},{1,0},{2,3},{3,2},{4,5},{5,4},{6,7},{7,6},{8,9},{9,8},{10,11... | collective-permute-start | bytes 2359304 | tf_op jit(solution)/shard_map/ppermute | solution.py:26
  41.7 1.8 %copy-start = (bf16[1024,512]{1,0:T(8,128)(2,1)S(1)}, bf16[1024,512]{1,0:T(8,128)(2,1)}, u32[]{:S(2)}) copy-start(bf16[1024,512]{1,0:T(8,128)(2,1)} %own.1) | copy-start | bytes 3145732
  55.3 11.3 %collective-permute-start.15 = (bf16[368,512]{1,0:T(8,128)(2,1)S(1)}, bf16[368,512]{1,0:T(8,128)(2,1)S(1)}, u32[]{:S(2)}, u32[]{:S(2)}) collective-permute-start(bf16[368,512]{1,0:T(8,128)(2,1)S(1)} %slice.11), channel_id=1, source_target_pairs={{0,96},{32,64},{64,32},{96,0},{128,224},{160,192},{192,160},{224,1... | collective-permute-start | bytes 1130504 | tf_op jit(solution)/shard_map/ppermute | solution.py:22
  56.5 9.7 %collective-permute-start.13 = (bf16[352,512]{1,0:T(8,128)(2,1)S(1)}, bf16[352,512]{1,0:T(8,128)(2,1)S(1)}, u32[]{:S(2)}, u32[]{:S(2)}) collective-permute-start(bf16[352,512]{1,0:T(8,128)(2,1)S(1)} %slice.9), channel_id=1, source_target_pairs={{0,128},{32,160},{64,192},{96,224},{128,0},{160,32},{192,64},{224,... | collective-permute-start | bytes 1081352 | tf_op jit(solution)/shard_map/ppermute | solution.py:22
  58.6 7.7 %collective-permute-start.14 = (bf16[304,512]{1,0:T(8,128)(2,1)S(1)}, bf16[304,512]{1,0:T(8,128)(2,1)S(1)}, u32[]{:S(2)}, u32[]{:S(2)}) collective-permute-start(bf16[304,512]{1,0:T(8,128)(2,1)S(1)} %slice.10), channel_id=1, source_target_pairs={{0,32},{32,0},{64,96},{96,64},{128,160},{160,128},{192,224},{224,1... | collective-permute-start | bytes 933896 | tf_op jit(solution)/shard_map/ppermute | solution.py:22

commit v3 on v1

--- a/solution.py
+++ b/solution.py
@@ -167,7 +167,7 @@
 
     sent, packed = barrier((amps, packed))
     p1 = row_flip(sent, 4)
-    pair = call(join_kernel, (packed, col_flip(packed, 2)), (2, TILE, 2 * TILE), BF16, "pair", flops=20000000000)
+    pair = call(join_kernel, (packed, col_flip(packed, 2)), (2, TILE, 2 * TILE), BF16, "pair", flops=20000000000, limit=60)
     quad = call(join_kernel, (pair, col_flip(pair, 1)), (4, TILE, 2 * TILE), BF16, "quad")
     r1, r2 = barrier((z_step(quad, 1), z_step(quad, 2)))
     p1, q1, w1 = barrier((p1, q1, w1))

time: 68.3 us -> 71 us (1.040)
  starting transfers between devices: 23.2 us -> 25.2 us
  waiting for transfers between devices: 27.6 us -> 26.1 us
  Pallas kernels: 16.2 us -> 17.6 us
    ppermute x9, waiting for transfers between devices: 14.2 us -> 11.3 us  [row_flip(): return lax.ppermute(value, 'row', [(i, i ^ flip) for i in range(8)])]
    ppermute x9, starting transfers between devices: 10.2 us -> 12.3 us  [row_flip(): return lax.ppermute(value, 'row', [(i, i ^ flip) for i in range(8)])]
    pallas_call x9, Pallas kernels: 16.2 us -> 17.6 us  [call(): pl.pallas_call(kernel, in_specs=[spec(SMEM)] * table + [spec(VMEM)] * (le...]
    ppermute x4, waiting for transfers between devices: 12 us -> 13.2 us  [z_step(): lax.ppermute(value, 'col', [(i, (i + (4 * by if i % 2 == 0 else -4 * by))...]
    unnamed x6 -> x8, local copies, waits for them, and re-layouts: 0.85 us -> 1.53 us
  transfers between devices with their start and end apart: 16 -> 16, of which waited for: 9 -> 8; matrix products, arithmetic and copies ran while one was open for 0% -> 0% of each run, Pallas kernels for 18% -> 20%
where the time goes in v3:
time: 71 us; the launch traced here: 70.8 us
  waiting for transfers between devices  26.1 us (37%)
  starting transfers between devices  25.2 us (35%)
  Pallas kernels  17.6 us (25%)
  local copies, waits for them, and re-layouts  1.6 us (2%)
    pallas_call x9, Pallas kernels, call(): pl.pallas_call(kernel, in_specs=[spec(SMEM)] * table + [spec(VMEM)] * (le...  17.6 us
    ppermute x4, waiting for transfers between devices, z_step(): lax.ppermute(value, 'col', [(i, (i + (4 * by if i % 2 == 0 else -4 * by))...  13.2 us
    ppermute x9, starting transfers between devices, row_flip(): return lax.ppermute(value, 'row', [(i, i ^ flip) for i in range(8)])  12.3 us
    ppermute x9, waiting for transfers between devices, row_flip(): return lax.ppermute(value, 'row', [(i, i ^ flip) for i in range(8)])  11.3 us
    ppermute x4, starting transfers between devices, z_step(): lax.ppermute(value, 'col', [(i, (i + (4 * by if i % 2 == 0 else -4 * by))...  9.78 us
    ppermute x3, starting transfers between devices, col_flip(): return lax.ppermute(value, 'col', [(i, i ^ flip) for i in range(32)])  3.12 us
    ppermute x3, waiting for transfers between devices, col_flip(): return lax.ppermute(value, 'col', [(i, i ^ flip) for i in range(32)])  1.56 us
    unnamed x8, local copies, waits for them, and re-layouts  1.53 us
  transfers between devices with their start and end apart: 16, of which 8 were waited for; matrix products, arithmetic and copies ran while one was open for 0% of the time, Pallas kernels for 20%

profile of v3, /device:TPU:64, one launch (start us, length us, event | category | flops | bytes accessed | tf_op | source)
XLA Modules:
  0.0 70.8 jit_solution(10897057479058827865)
XLA Ops:
  0.0 1.6 %pack.1.a = bf16[128,256]{1,0:T(8,128)(2,1)} custom-call(s32[32,64]{1,0:T(8,128)} %mask_ref.3, bf16[128,1024]{1,0:T(8,128)(2,1)} %v_ref.1), custom_call_target="tpu_custom_call" | custom-call | flops 1000 | bytes 1000 | tf_op jit(solution)/shard_map/pack/pallas_call | solution.py:149
  1.6 0.0 copy-start.2
  1.6 3.0 %collective-permute-start = (bf16[128,256]{1,0:T(8,128)(2,1)}, bf16[128,256]{1,0:T(8,128)(2,1)S(1)}, u32[]{:S(2)}, u32[]{:S(2)}) collective-permute-start(bf16[128,256]{1,0:T(8,128)(2,1)} %pack.1.a), channel_id=1, source_target_pairs={{0,2},{1,3},{2,0},{3,1},{4,6},{5,7},{6,4},{7,5},{8,10},{9,11},{10,... | collective-permute-start | bytes 196616 | tf_op jit(solution)/shard_map/ppermute | solution.py:26
  4.7 1.6 %collective-permute-start.8 = (bf16[1024,512]{1,0:T(8,128)(2,1)}, bf16[1024,512]{1,0:T(8,128)(2,1)S(1)}, u32[]{:S(2)}, u32[]{:S(2)}) collective-permute-start(bf16[1024,512]{1,0:T(8,128)(2,1)} %own.1), channel_id=1, source_target_pairs={{0,32},{32,0},{64,96},{96,64},{128,160},{160,128},{192,224},{224,1... | collective-permute-start | bytes 3145736 | tf_op jit(solution)/shard_map/ppermute | solution.py:22
  6.2 2.2 %collective-permute-start.9 = (bf16[1024,512]{1,0:T(8,128)(2,1)}, bf16[1024,512]{1,0:T(8,128)(2,1)S(1)}, u32[]{:S(2)}, u32[]{:S(2)}) collective-permute-start(bf16[1024,512]{1,0:T(8,128)(2,1)} %own.1), channel_id=1, source_target_pairs={{0,96},{32,64},{64,32},{96,0},{128,224},{160,192},{192,160},{224,1... | collective-permute-start | bytes 3145736 | tf_op jit(solution)/shard_map/ppermute | solution.py:22
  8.4 0.6 collective-permute-start.7
  9.0 0.0 collective-permute-done.b
  9.0 0.0 copy-start.3
  9.0 0.6 copy-done.3
  9.6 1.5 %pair.1.a = bf16[2,128,256]{2,1,0:T(8,128)(2,1)} custom-call(bf16[128,256]{1,0:T(8,128)(2,1)} %pack.1.a, bf16[128,256]{1,0:T(8,128)(2,1)} %copy-done.3), custom_call_target="tpu_custom_call" | custom-call | flops 20000000000 | bytes 1000 | tf_op jit(solution)/shard_map/pair/pallas_call | solution.py:149
  11.2 0.0 collective-permute-start.1
  11.2 1.6 %collective-permute-done.1.b = bf16[2,128,256]{2,1,0:T(8,128)(2,1)S(1)} collective-permute-done((bf16[2,128,256]{2,1,0:T(8,128)(2,1)}, bf16[2,128,256]{2,1,0:T(8,128)(2,1)S(1)}, u32[]{:S(2)}, u32[]{:S(2)}) %collective-permute-start.1) | collective-permute-done | bytes 131104 | tf_op jit(solution)/shard_map/ppermute | solution.py:26
  12.7 0.0 copy-start.1
  12.7 0.9 %copy-done.1 = bf16[2,128,256]{2,1,0:T(8,128)(2,1)S(1)} copy-done((bf16[2,128,256]{2,1,0:T(8,128)(2,1)S(1)}, bf16[2,128,256]{2,1,0:T(8,128)(2,1)}, u32[]{:S(2)}) %copy-start.1) | copy-done | bytes 131096
  13.7 4.6 %collective-permute-start.3 = (bf16[4,128,256]{2,1,0:T(8,128)(2,1)S(1)}, bf16[4,128,256]{2,1,0:T(8,128)(2,1)S(1)}, u32[]{:S(2)}, u32[]{:S(2)}) collective-permute-start(bf16[4,128,256]{2,1,0:T(8,128)(2,1)S(1)} %quad.1), channel_id=1, source_target_pairs={{0,8},{1,25},{2,10},{3,27},{4,12},{5,29},{6,14},{7,31},{8,16},{9,1... | collective-permute-start | bytes 786440 | tf_op jit(solution)/shard_map/ppermute | solution.py:30
  18.2 1.0 %collective-permute-start.2 = (bf16[4,128,256]{2,1,0:T(8,128)(2,1)S(1)}, bf16[4,128,256]{2,1,0:T(8,128)(2,1)S(1)}, u32[]{:S(2)}, u32[]{:S(2)}) collective-permute-start(bf16[4,128,256]{2,1,0:T(8,128)(2,1)S(1)} %quad.1), channel_id=1, source_target_pairs={{0,4},{1,29},{2,6},{3,31},{4,8},{5,1},{6,10},{7,3},{8,12},{9,5},{1... | collective-permute-start | bytes 786440 | tf_op jit(solution)/shard_map/ppermute | solution.py:30
  19.2 5.6 %collective-permute-done.3.b.r2 = bf16[4,128,256]{2,1,0:T(8,128)(2,1)S(1)} collective-permute-done((bf16[4,128,256]{2,1,0:T(8,128)(2,1)S(1)}, bf16[4,128,256]{2,1,0:T(8,128)(2,1)S(1)}, u32[]{:S(2)}, u32[]{:S(2)}) %collective-permute-start.3) | collective-permute-done | bytes 262176 | tf_op jit(solution)/shard_map/ppermute | solution.py:30
  24.9 2.8 %collective-permute-done.2.a.r1 = bf16[4,128,256]{2,1,0:T(8,128)(2,1)S(1)} collective-permute-done((bf16[4,128,256]{2,1,0:T(8,128)(2,1)S(1)}, bf16[4,128,256]{2,1,0:T(8,128)(2,1)S(1)}, u32[]{:S(2)}, u32[]{:S(2)}) %collective-permute-start.2) | collective-permute-done | bytes 262176 | tf_op jit(solution)/shard_map/ppermute | solution.py:30
  27.7 4.2 %collective-permute-start.5 = (bf16[4,128,256]{2,1,0:T(8,128)(2,1)S(1)}, bf16[4,128,256]{2,1,0:T(8,128)(2,1)S(1)}, u32[]{:S(2)}, u32[]{:S(2)}) collective-permute-start(bf16[4,128,256]{2,1,0:T(8,128)(2,1)S(1)} %collective-permute-done.3.b.r2), channel_id=1, source_target_pairs={{0,8},{1,25},{2,10},{3,27},{4,12},{5,29},{6,14},{7,31},{8,16},{9,1... | collective-permute-start | bytes 786440 | tf_op jit(solution)/shard_map/ppermute | solution.py:30
  31.9 0.0 collective-permute-start.4
  31.9 0.8 %collective-permute-done.7.p1 = bf16[1024,512]{1,0:T(8,128)(2,1)S(1)} collective-permute-done((bf16[1024,512]{1,0:T(8,128)(2,1)}, bf16[1024,512]{1,0:T(8,128)(2,1)S(1)}, u32[]{:S(2)}, u32[]{:S(2)}) %collective-permute-start.7) | collective-permute-done | bytes 1048608 | tf_op jit(solution)/shard_map/ppermute | solution.py:22
  32.7 0.0 collective-permute-done.8.q1
  32.7 0.0 collective-permute-done.9.w1
  32.7 0.7 collective-permute-start.11
  33.4 1.0 %collective-permute-start.12 = (bf16[1024,512]{1,0:T(8,128)(2,1)S(1)}, bf16[1024,512]{1,0:T(8,128)(2,1)S(1)}, u32[]{:S(2)}, u32[]{:S(2)}) collective-permute-start(bf16[1024,512]{1,0:T(8,128)(2,1)S(1)} %collective-permute-done.8.q1), channel_id=1, source_target_pairs={{0,96},{32,64},{64,32},{96,0},{128,224},{160,192},{192,160},{224,1... | collective-permute-start | bytes 3145736 | tf_op jit(solution)/shard_map/ppermute | solution.py:22
  34.4 2.2 %collective-permute-start.10 = (bf16[1024,512]{1,0:T(8,128)(2,1)S(1)}, bf16[1024,512]{1,0:T(8,128)(2,1)S(1)}, u32[]{:S(2)}, u32[]{:S(2)}) collective-permute-start(bf16[1024,512]{1,0:T(8,128)(2,1)S(1)} %collective-permute-done.9.w1), channel_id=1, source_target_pairs={{0,128},{32,160},{64,192},{96,224},{128,0},{160,32},{192,64},{224,... | collective-permute-start | bytes 3145736 | tf_op jit(solution)/shard_map/ppermute | solution.py:22
  36.5 1.3 %collective-permute-done.5.r4 = bf16[4,128,256]{2,1,0:T(8,128)(2,1)S(1)} collective-permute-done((bf16[4,128,256]{2,1,0:T(8,128)(2,1)S(1)}, bf16[4,128,256]{2,1,0:T(8,128)(2,1)S(1)}, u32[]{:S(2)}, u32[]{:S(2)}) %collective-permute-start.5) | collective-permute-done | bytes 262176 | tf_op jit(solution)/shard_map/ppermute | solution.py:30
  37.9 3.5 %collective-permute-done.4.c.r3 = bf16[4,128,256]{2,1,0:T(8,128)(2,1)S(1)} collective-permute-done((bf16[4,128,256]{2,1,0:T(8,128)(2,1)S(1)}, bf16[4,128,256]{2,1,0:T(8,128)(2,1)S(1)}, u32[]{:S(2)}, u32[]{:S(2)}) %collective-permute-start.4) | collective-permute-done | bytes 262176 | tf_op jit(solution)/shard_map/ppermute | solution.py:30
  41.3 0.1 three.1
  41.4 0.1 collective-permute-start.6
  41.5 0.0 copy-done.2
  41.5 2.5 %table.1.table_ref = s32[2,32]{1,0:T(2,128)S(1)} custom-call(s32[32,64]{1,0:T(8,128)S(1)} %copy-done.2), custom_call_target="tpu_custom_call" | custom-call | flops 1000 | bytes 1000 | tf_op jit(solution)/shard_map/table/pallas_call | solution.py:149
  44.0 0.0 copy-start
  44.0 0.0 collective-permute-done.6.theirs
  44.0 1.7 %dense.1.dense_ref = bf16[4096,1024]{1,0:T(8,128)(2,1)S(1)} custom-call(s32[2,32]{1,0:T(2,128)S(1)} %table.1.table_ref, bf16[4,128,256]{2,1,0:T(8,128)(2,1)S(1)} %quad.1, bf16[4,128,256]{2,1,0:T(8,128)(2,1)S(1)} %collective-permute-done.2.a.r1, bf16[4,128,256]{2,1,0:T(8,128)(2,1)S(1)} %collective-permute-done.3.b.r2, ...), custom_call_target="tpu_custom_call" | custom-call | flops 2000000000 | bytes 1000 | tf_op jit(solution)/shard_map/dense/pallas_call | solution.py:149
  45.7 0.0 copy-done
  45.7 4.5 %first.1.acc_in = f32[1024,1024]{1,0:T(8,128)S(1)} custom-call(bf16[4096,1024]{1,0:T(8,128)(2,1)S(1)} %dense.1.dense_ref, bf16[1024,512]{1,0:T(8,128)(2,1)S(1)} %copy-done, bf16[1024,512]{1,0:T(8,128)(2,1)S(1)} %collective-permute-done.7.p1, bf16[1024,512]{1,0:T(8,128)(2,1)S(1)} %collective-permute-done.8.q1, bf16[1024,512]{1,0:T(8,128)(2,1)S(1)} %collective-permute-done.9.w1), custom_call_target="tpu_custom_call" | custom-call | flops 1000 | bytes 1000 | tf_op jit(solution)/shard_map/first/pallas_call | solution.py:149
  50.3 6.5 %collective-permute-done.11.qp = bf16[1024,512]{1,0:T(8,128)(2,1)S(1)} collective-permute-done((bf16[1024,512]{1,0:T(8,128)(2,1)S(1)}, bf16[1024,512]{1,0:T(8,128)(2,1)S(1)}, u32[]{:S(2)}, u32[]{:S(2)}) %collective-permute-start.11) | collective-permute-done | bytes 1048608 | tf_op jit(solution)/shard_map/ppermute | solution.py:22
  56.8 1.7 %collective-permute-start.15 = (bf16[368,512]{1,0:T(8,128)(2,1)S(1)}, bf16[368,512]{1,0:T(8,128)(2,1)S(1)}, u32[]{:S(2)}, u32[]{:S(2)}) collective-permute-start(bf16[368,512]{1,0:T(8,128)(2,1)S(1)} %slice.11), channel_id=1, source_target_pairs={{0,96},{32,64},{64,32},{96,0},{128,224},{160,192},{192,160},{224,1... | collective-permute-start | bytes 1130504 | tf_op jit(solution)/shard_map/ppermute | solution.py:22
  58.5 0.0 collective-permute-done.12.wq
  58.6 2.3 %collective-permute-start.13 = (bf16[352,512]{1,0:T(8,128)(2,1)S(1)}, bf16[352,512]{1,0:T(8,128)(2,1)S(1)}, u32[]{:S(2)}, u32[]{:S(2)}) collective-permute-start(bf16[352,512]{1,0:T(8,128)(2,1)S(1)} %slice.9), channel_id=1, source_target_pairs={{0,128},{32,160},{64,192},{96,224},{128,0},{160,32},{192,64},{224,... | collective-permute-start | bytes 1081352 | tf_op jit(solution)/shard_map/ppermute | solution.py:22
  60.9 0.0 collective-permute-done.10.pw
  60.9 0.1 collective-permute-start.14
  61.0 3.5 %second.1.acc_ref = f32[1024,1024]{1,0:T(8,128)S(1)} custom-call(bf16[4096,1024]{1,0:T(8,128)(2,1)S(1)} %dense.1.dense_ref, f32[1024,1024]{1,0:T(8,128)S(1)} %first.1.acc_in, bf16[1024,512]{1,0:T(8,128)(2,1)S(1)} %collective-permute-done.10.pw, bf16[1024,512]{1,0:T(8,128)(2,1)S(1)} %collective-permute-done.11.qp, ...), custom_call_target="tpu_custom_call", output_to_operand_aliasing={{}: (1, {})} | custom-call | flops 1000 | bytes 1000 | tf_op jit(solution)/shard_map/second/pallas_call | solution.py:149
  64.6 4.0 %collective-permute-done.14.tb = bf16[304,512]{1,0:T(8,128)(2,1)S(1)} collective-permute-done((bf16[304,512]{1,0:T(8,128)(2,1)S(1)}, bf16[304,512]{1,0:T(8,128)(2,1)S(1)}, u32[]{:S(2)}, u32[]{:S(2)}) %collective-permute-start.14) | collective-permute-done | bytes 311328 | tf_op jit(solution)/shard_map/ppermute | solution.py:22
  68.6 0.0 collective-permute-done.13.ta
  68.6 0.0 collective-permute-done.15.tc
  68.6 2.1 %third.1 = bf16[1024,1024]{1,0:T(8,128)(2,1)} custom-call(bf16[4096,1024]{1,0:T(8,128)(2,1)S(1)} %dense.1.dense_ref, f32[1024,1024]{1,0:T(8,128)S(1)} %second.1.acc_ref, bf16[352,512]{1,0:T(8,128)(2,1)S(1)} %collective-permute-done.13.ta, bf16[304,512]{1,0:T(8,128)(2,1)S(1)} %collective-permute-done.14.tb, bf16[368,512]{1,0:T(8,128)(2,1)S(1)} %collective-permute-done.15.tc), custom_call_target="tpu_custom_call" | custom-call | flops 1000 | bytes 1000 | tf_op jit(solution)/shard_map/third/pallas_call | solution.py:149
  (4 shorter events, 0.1 us)
Async XLA Ops:
  1.6 39.8 %copy-start.2 = (s32[32,64]{1,0:T(8,128)S(1)}, s32[32,64]{1,0:T(8,128)}, u32[]{:S(2)}) copy-start(s32[32,64]{1,0:T(8,128)} %mask_ref.3) | copy-start | bytes 24580
  1.6 7.4 %collective-permute-start = (bf16[128,256]{1,0:T(8,128)(2,1)}, bf16[128,256]{1,0:T(8,128)(2,1)S(1)}, u32[]{:S(2)}, u32[]{:S(2)}) collective-permute-start(bf16[128,256]{1,0:T(8,128)(2,1)} %pack.1.a), channel_id=1, source_target_pairs={{0,2},{1,3},{2,0},{3,1},{4,6},{5,7},{6,4},{7,5},{8,10},{9,11},{10,... | collective-permute-start | bytes 196616 | tf_op jit(solution)/shard_map/ppermute | solution.py:26
  4.7 28.0 %collective-permute-start.8 = (bf16[1024,512]{1,0:T(8,128)(2,1)}, bf16[1024,512]{1,0:T(8,128)(2,1)S(1)}, u32[]{:S(2)}, u32[]{:S(2)}) collective-permute-start(bf16[1024,512]{1,0:T(8,128)(2,1)} %own.1), channel_id=1, source_target_pairs={{0,32},{32,0},{64,96},{96,64},{128,160},{160,128},{192,224},{224,1... | collective-permute-start | bytes 3145736 | tf_op jit(solution)/shard_map/ppermute | solution.py:22
  6.2 26.5 %collective-permute-start.9 = (bf16[1024,512]{1,0:T(8,128)(2,1)}, bf16[1024,512]{1,0:T(8,128)(2,1)S(1)}, u32[]{:S(2)}, u32[]{:S(2)}) collective-permute-start(bf16[1024,512]{1,0:T(8,128)(2,1)} %own.1), channel_id=1, source_target_pairs={{0,96},{32,64},{64,32},{96,0},{128,224},{160,192},{192,160},{224,1... | collective-permute-start | bytes 3145736 | tf_op jit(solution)/shard_map/ppermute | solution.py:22
  8.4 24.3 %collective-permute-start.7 = (bf16[1024,512]{1,0:T(8,128)(2,1)}, bf16[1024,512]{1,0:T(8,128)(2,1)S(1)}, u32[]{:S(2)}, u32[]{:S(2)}) collective-permute-start(bf16[1024,512]{1,0:T(8,128)(2,1)} %own.1), channel_id=1, source_target_pairs={{0,128},{32,160},{64,192},{96,224},{128,0},{160,32},{192,64},{224,... | collective-permute-start | bytes 3145736 | tf_op jit(solution)/shard_map/ppermute | solution.py:22
  9.0 0.6 copy-start.3
  11.2 1.6 %collective-permute-start.1 = (bf16[2,128,256]{2,1,0:T(8,128)(2,1)}, bf16[2,128,256]{2,1,0:T(8,128)(2,1)S(1)}, u32[]{:S(2)}, u32[]{:S(2)}) collective-permute-start(bf16[2,128,256]{2,1,0:T(8,128)(2,1)} %pair.1.a), channel_id=1, source_target_pairs={{0,1},{1,0},{2,3},{3,2},{4,5},{5,4},{6,7},{7,6},{8,9},{9,8},{10,11... | collective-permute-start | bytes 393224 | tf_op jit(solution)/shard_map/ppermute | solution.py:26
  12.7 0.9 %copy-start.1 = (bf16[2,128,256]{2,1,0:T(8,128)(2,1)S(1)}, bf16[2,128,256]{2,1,0:T(8,128)(2,1)}, u32[]{:S(2)}) copy-start(bf16[2,128,256]{2,1,0:T(8,128)(2,1)} %pair.1.a) | copy-start | bytes 393220
  13.7 11.2 %collective-permute-start.3 = (bf16[4,128,256]{2,1,0:T(8,128)(2,1)S(1)}, bf16[4,128,256]{2,1,0:T(8,128)(2,1)S(1)}, u32[]{:S(2)}, u32[]{:S(2)}) collective-permute-start(bf16[4,128,256]{2,1,0:T(8,128)(2,1)S(1)} %quad.1), channel_id=1, source_target_pairs={{0,8},{1,25},{2,10},{3,27},{4,12},{5,29},{6,14},{7,31},{8,16},{9,1... | collective-permute-start | bytes 786440 | tf_op jit(solution)/shard_map/ppermute | solution.py:30
  18.2 9.5 %collective-permute-start.2 = (bf16[4,128,256]{2,1,0:T(8,128)(2,1)S(1)}, bf16[4,128,256]{2,1,0:T(8,128)(2,1)S(1)}, u32[]{:S(2)}, u32[]{:S(2)}) collective-permute-start(bf16[4,128,256]{2,1,0:T(8,128)(2,1)S(1)} %quad.1), channel_id=1, source_target_pairs={{0,4},{1,29},{2,6},{3,31},{4,8},{5,1},{6,10},{7,3},{8,12},{9,5},{1... | collective-permute-start | bytes 786440 | tf_op jit(solution)/shard_map/ppermute | solution.py:30
  27.7 10.2 %collective-permute-start.5 = (bf16[4,128,256]{2,1,0:T(8,128)(2,1)S(1)}, bf16[4,128,256]{2,1,0:T(8,128)(2,1)S(1)}, u32[]{:S(2)}, u32[]{:S(2)}) collective-permute-start(bf16[4,128,256]{2,1,0:T(8,128)(2,1)S(1)} %collective-permute-done.3.b.r2), channel_id=1, source_target_pairs={{0,8},{1,25},{2,10},{3,27},{4,12},{5,29},{6,14},{7,31},{8,16},{9,1... | collective-permute-start | bytes 786440 | tf_op jit(solution)/shard_map/ppermute | solution.py:30
  31.9 9.4 %collective-permute-start.4 = (bf16[4,128,256]{2,1,0:T(8,128)(2,1)S(1)}, bf16[4,128,256]{2,1,0:T(8,128)(2,1)S(1)}, u32[]{:S(2)}, u32[]{:S(2)}) collective-permute-start(bf16[4,128,256]{2,1,0:T(8,128)(2,1)S(1)} %collective-permute-done.3.b.r2), channel_id=1, source_target_pairs={{0,4},{1,29},{2,6},{3,31},{4,8},{5,1},{6,10},{7,3},{8,12},{9,5},{1... | collective-permute-start | bytes 786440 | tf_op jit(solution)/shard_map/ppermute | solution.py:30
  32.7 24.1 %collective-permute-start.11 = (bf16[1024,512]{1,0:T(8,128)(2,1)S(1)}, bf16[1024,512]{1,0:T(8,128)(2,1)S(1)}, u32[]{:S(2)}, u32[]{:S(2)}) collective-permute-start(bf16[1024,512]{1,0:T(8,128)(2,1)S(1)} %collective-permute-done.7.p1), channel_id=1, source_target_pairs={{0,32},{32,0},{64,96},{96,64},{128,160},{160,128},{192,224},{224,1... | collective-permute-start | bytes 3145736 | tf_op jit(solution)/shard_map/ppermute | solution.py:22
  33.4 25.1 %collective-permute-start.12 = (bf16[1024,512]{1,0:T(8,128)(2,1)S(1)}, bf16[1024,512]{1,0:T(8,128)(2,1)S(1)}, u32[]{:S(2)}, u32[]{:S(2)}) collective-permute-start(bf16[1024,512]{1,0:T(8,128)(2,1)S(1)} %collective-permute-done.8.q1), channel_id=1, source_target_pairs={{0,96},{32,64},{64,32},{96,0},{128,224},{160,192},{192,160},{224,1... | collective-permute-start | bytes 3145736 | tf_op jit(solution)/shard_map/ppermute | solution.py:22
  34.4 26.5 %collective-permute-start.10 = (bf16[1024,512]{1,0:T(8,128)(2,1)S(1)}, bf16[1024,512]{1,0:T(8,128)(2,1)S(1)}, u32[]{:S(2)}, u32[]{:S(2)}) collective-permute-start(bf16[1024,512]{1,0:T(8,128)(2,1)S(1)} %collective-permute-done.9.w1), channel_id=1, source_target_pairs={{0,128},{32,160},{64,192},{96,224},{128,0},{160,32},{192,64},{224,... | collective-permute-start | bytes 3145736 | tf_op jit(solution)/shard_map/ppermute | solution.py:22
  41.4 2.6 %collective-permute-start.6 = (bf16[12,128,256]{2,1,0:T(8,128)(2,1)S(1)}, bf16[12,128,256]{2,1,0:T(8,128)(2,1)S(1)}, u32[]{:S(2)}, u32[]{:S(2)}) collective-permute-start(bf16[12,128,256]{2,1,0:T(8,128)(2,1)S(1)} %three.1), channel_id=1, source_target_pairs={{0,1},{1,0},{2,3},{3,2},{4,5},{5,4},{6,7},{7,6},{8,9},{9,8},{10,11... | collective-permute-start | bytes 2359304 | tf_op jit(solution)/shard_map/ppermute | solution.py:26
  44.0 1.8 %copy-start = (bf16[1024,512]{1,0:T(8,128)(2,1)S(1)}, bf16[1024,512]{1,0:T(8,128)(2,1)}, u32[]{:S(2)}) copy-start(bf16[1024,512]{1,0:T(8,128)(2,1)} %own.1) | copy-start | bytes 3145732
  56.8 11.7 %collective-permute-start.15 = (bf16[368,512]{1,0:T(8,128)(2,1)S(1)}, bf16[368,512]{1,0:T(8,128)(2,1)S(1)}, u32[]{:S(2)}, u32[]{:S(2)}) collective-permute-start(bf16[368,512]{1,0:T(8,128)(2,1)S(1)} %slice.11), channel_id=1, source_target_pairs={{0,96},{32,64},{64,32},{96,0},{128,224},{160,192},{192,160},{224,1... | collective-permute-start | bytes 1130504 | tf_op jit(solution)/shard_map/ppermute | solution.py:22
  58.6 10.0 %collective-permute-start.13 = (bf16[352,512]{1,0:T(8,128)(2,1)S(1)}, bf16[352,512]{1,0:T(8,128)(2,1)S(1)}, u32[]{:S(2)}, u32[]{:S(2)}) collective-permute-start(bf16[352,512]{1,0:T(8,128)(2,1)S(1)} %slice.9), channel_id=1, source_target_pairs={{0,128},{32,160},{64,192},{96,224},{128,0},{160,32},{192,64},{224,... | collective-permute-start | bytes 1081352 | tf_op jit(solution)/shard_map/ppermute | solution.py:22
  60.9 7.6 %collective-permute-start.14 = (bf16[304,512]{1,0:T(8,128)(2,1)S(1)}, bf16[304,512]{1,0:T(8,128)(2,1)S(1)}, u32[]{:S(2)}, u32[]{:S(2)}) collective-permute-start(bf16[304,512]{1,0:T(8,128)(2,1)S(1)} %slice.10), channel_id=1, source_target_pairs={{0,32},{32,0},{64,96},{96,64},{128,160},{160,128},{192,224},{224,1... | collective-permute-start | bytes 933896 | tf_op jit(solution)/shard_map/ppermute | solution.py:22
